TPU v7x, 128 devices: a whole 4x4x4 slice. The times are simulated.
128 devices in a mesh: row: 8 (over x, z_lo), col: 16 (over y, z_hi, core).
Axes of the slice: x: 4, y: 4, z: 4 (z_hi: 2, z_lo: 2; z = z_hi * 2 + z_lo), core: 2. Of those that a mesh axis runs over, the one named last changes fastest.
Arguments:
- momentum: bfloat16 [16384, 16384], P('row', 'col'), may hold values from -6 to 6
- gradient: bfloat16 [16384, 16384], P('row', 'col'), may hold values from -43 to 43
- right_prev: float32 [16384, 512], P('col'), may hold values from -6 to 6
- weight: bfloat16 [16384, 16384], P('col', 'row'), may hold values from -0.046875 to 0.046875
- tokens: bfloat16 [256, 16384], P(None, 'row'), may hold values from -6 to 6
Outputs:
- new_momentum: bfloat16 [16384, 16384], P('row', 'col')
- new_basis: float32 [16384, 512], P('col')
- new_weight: bfloat16 [16384, 16384], P('col', 'row')
- projected: bfloat16 [256, 16384], P('row', 'col')
All inputs are finite; a program needn't handle non-finite values.
Results may differ from a plain program's by a relative error of at most 0.006.
Values may be sent and summed in bfloat16 or wider, within the bound.
No kernel may reach another device: no remote copies, remote signals or barrier semaphores. Data moves between devices by JAX's collectives and lax.ppermute only.
A program may use at most 128 MiB of HBM per device.

v0:
```python
import jax
import jax.numpy as jnp
from jax import lax
from jax.experimental import pallas as pl
from jax.experimental.pallas import tpu as pltpu
from jax.sharding import Mesh
from jax.sharding import PartitionSpec as P

DIN = 16384
COL = ("col_0", "col_1", "col_2")
ROW = ("row_0", "row_1")
ALL = ROW + COL
CORE = "col_2"
CHIPS = ("col_0", "col_1")

decay_part = 0.05
step_size = 0.01
epsilon = 1e-06

HIGH = lax.Precision.HIGH
HIGHEST = lax.Precision.HIGHEST


def whole(v):
    return jnp.broadcast_to(v, (8, 128))


def eliminate(z_ref, u_ref):
    lane = lax.broadcasted_iota(jnp.int32, (8, 128), 1)
    sub = lax.broadcasted_iota(jnp.int32, (8, 128), 0)
    rows = [[z_ref[t, 8 * q:8 * q + 8, :] for t in range(4)] for q in range(16)]
    for p in range(16):
        columns = {}
        for q in range(p, 16):
            for i in range(8):
                columns[q, i] = whole(rows[q][0][:, 8 * p + i:8 * p + i + 1])
        pivot = {(i, j): whole(columns[p, j][i:i + 1, :]) for j in range(8) for i in range(j, 8)}
        own = (lane >= 8 * p) & (lane < 8 * p + 8)
        start = [jnp.where(own, jnp.where(sub == lane - 8 * p, 1.0, 0.0), rows[p][0])] + rows[p][1:]
        inv = {}
        low = {}
        for j in range(8):
            r = lax.rsqrt(pivot[j, j])
            col = {i: pivot[i, j] * r for i in range(j + 1, 8)}
            for k in range(j + 1, 8):
                for i in range(k, 8):
                    pivot[i, k] = pivot[i, k] - col[i] * col[k]
            for m in range(j):
                inv[j, m] = pivot[j, m, "sum"] * (-r)
            inv[j, j] = r
            for i in range(j + 1, 8):
                for m in range(j + 1):
                    term = col[i] * inv[j, m]
                    pivot[i, m, "sum"] = term if m == j else pivot[i, m, "sum"] + term
        first = [[whole(start[t][i:i + 1, :]) for i in range(8)] for t in range(4)]
        solved = []
        for t in range(4):
            lows = []
            for i in range(8):
                v = inv[i, 0] * first[t][0]
                for m in range(1, i + 1):
                    v = v + inv[i, m] * first[t][m]
                lows.append(v)
            out = lows[0]
            for i in range(1, 8):
                out = jnp.where(sub == i, lows[i], out)
            u_ref[t, 8 * p:8 * p + 8, :] = jnp.where(lane <= sub + 8 * p, out, 0.0) if t == 0 else out
            line = []
            for i in range(8):
                v = inv[7, i] * lows[7]
                for m in range(i, 7):
                    v = v + inv[m, i] * lows[m]
                line.append(v)
            solved.append(line)
        for q in range(p + 1, 16):
            for t in range(4):
                total = jnp.where(own, 0.0, rows[q][t]) if t == 0 else rows[q][t]
                for i in range(8):
                    total = total - columns[q, i] * solved[t][i]
                rows[q][t] = total

def factor_kernel(g_ref, x_ref, z_ref, d_ref, u_ref):
    z_ref[...] = g_ref[...]
    def step(k, carry):
        at = pl.multiple_of(k * 128, 128)
        places = [pl.multiple_of(lax.rem(k + t, 4) * 128, 128) for t in range(4)]
        for t in range(4):
            d_ref[t] = z_ref[pl.ds(at, 128), pl.ds(places[t], 128)]
        eliminate(d_ref, u_ref)
        for t in range(4):
            x_ref[pl.ds(at, 128), pl.ds(places[t], 128)] = jnp.where(places[t] <= at, u_ref[t], 0.0)
        for t in range(1, 4):
            @pl.when(places[t] > at)
            def _():
                lower = u_ref[t]
                rest = pl.ds(places[t], 128)
                for s in range(4):
                    change = lax.dot_general(lower, u_ref[s], (((0,), (0,)), ((), ())), precision=HIGHEST, preferred_element_type=jnp.float32)
                    if s == 0:
                        z_ref[rest, pl.ds(places[s], 128)] = -change
                    else:
                        z_ref[rest, pl.ds(places[s], 128)] -= change
        return carry
    lax.fori_loop(0, 4, step, 0)


def inverse_factor(gram):
    return pl.pallas_call(
        factor_kernel,
        out_shape=jax.ShapeDtypeStruct((512, 512), jnp.float32),
        scratch_shapes=[
            pltpu.VMEM((512, 512), jnp.float32),
            pltpu.VMEM((4, 128, 128), jnp.float32),
            pltpu.VMEM((4, 128, 128), jnp.float32),
        ],
        compiler_params=pltpu.CompilerParams(vmem_limit_bytes=16 * 1024 * 1024),
    )(gram)


def dot(lhs, rhs, dims, precision=None):
    return lax.dot_general(
        lhs, rhs, ((dims[:1], dims[1:]), ((), ())), precision=precision, preferred_element_type=jnp.float32
    )


def scatter_sum(array, axes, length):
    pieces = array.reshape(length, array.shape[0] // length, *array.shape[1:])
    return jnp.sum(lax.all_to_all(pieces, axes, 0, 0, tiled=True).astype(jnp.float32), axis=0)


def gathered(array, axes, length):
    pieces = lax.all_to_all(
        jnp.broadcast_to(array[None], (length, *array.shape)), axes, 0, 0, tiled=True
    )
    return pieces.reshape(length * array.shape[0], *array.shape[1:])


def to_other_core(array):
    return lax.ppermute(array, CORE, [(0, 1), (1, 0)])


def in_core_order(own, other, core):
    return jnp.where(
        core == 0, jnp.concatenate([own, other], axis=0), jnp.concatenate([other, own], axis=0)
    )


def to_tile_owner(array):
    pairs = [(r * 16 + 2 * j + k, j * 16 + 2 * r + k) for r in range(8) for j in range(8) for k in range(2)]
    return lax.ppermute(array, ALL, pairs)


def in_two_parts(row):
    first = row.astype(jnp.bfloat16)
    second = (row - first.astype(jnp.float32)).astype(jnp.bfloat16)
    index = lax.broadcasted_iota(jnp.int32, (16, row.shape[0]), 0)
    zero = jnp.zeros((), jnp.bfloat16)
    return jnp.where(index == 0, first[None], jnp.where(index == 1, second[None], zero))


def split(array):
    first = array.astype(jnp.bfloat16)
    return first, (array - first.astype(jnp.float32)).astype(jnp.bfloat16)


def project_kernel(core_ref, first_ref, second_ref, own_ref, other_ref, out_ref):
    step = pl.program_id(0)
    left = jnp.where(step < 4, own_ref[...], other_ref[...])
    high = left.astype(jnp.bfloat16)
    low = (left - high.astype(jnp.float32)).astype(jnp.bfloat16)
    first = first_ref[...]
    part = jnp.dot(first, high, preferred_element_type=jnp.float32)
    part += jnp.dot(first, low, preferred_element_type=jnp.float32)
    part += jnp.dot(second_ref[...], high, preferred_element_type=jnp.float32)

    @pl.when(step == 0)
    def _():
        out_ref[...] = part

    @pl.when(step > 0)
    def _():
        out_ref[...] += part


def transposed_product(core, splits, own, other):
    def column(step, core_ref):
        half = lax.rem(core_ref[0] + step // 4, 2)
        return 0, half * 4 + lax.rem(step, 4)

    spec = pl.BlockSpec((1024, 256), column)
    return pl.pallas_call(
        project_kernel,
        out_shape=jax.ShapeDtypeStruct((1024, 512), jnp.float32),
        grid_spec=pltpu.PrefetchScalarGridSpec(
            num_scalar_prefetch=1,
            grid=(8,),
            in_specs=[
                spec,
                spec,
                pl.BlockSpec((256, 512), lambda step, core_ref: (jnp.minimum(step, 3), 0)),
                pl.BlockSpec((256, 512), lambda step, core_ref: (jnp.maximum(step - 4, 0), 0)),
            ],
            out_specs=pl.BlockSpec((1024, 512), lambda step, core_ref: (0, 0)),
        ),
        compiler_params=pltpu.CompilerParams(
            dimension_semantics=("arbitrary",), vmem_limit_bytes=24 * 1024 * 1024
        ),
    )(core[None], *splits, own, other)


def per_device(momentum, gradient, right_prev, weight, tokens):
    core = lax.axis_index(CORE)
    chip = lax.axis_index(CHIPS)

    def half(array, which):
        return lax.dynamic_slice_in_dim(array, which * 1024, 1024, 0)

    mixed = momentum.astype(jnp.float32) + gradient.astype(jnp.float32)
    partial_left = dot(mixed, right_prev, (1, 0), HIGH)
    partial_left = half(partial_left, core) + to_other_core(half(partial_left, 1 - core))
    partial_left, momentum, gradient = lax.optimization_barrier((partial_left, momentum, gradient))
    left_shard = scatter_sum(partial_left, CHIPS, 8)
    mixed_splits = split((momentum.astype(jnp.float32) + gradient.astype(jnp.float32)).T)
    left_shard, mixed_splits = lax.optimization_barrier((left_shard, mixed_splits))

    left_own = gathered(left_shard, CHIPS, 8)
    left_other = to_other_core(left_own)
    tile_left_raw = to_tile_owner(left_shard)

    gram_rows = core * 256 + chip * 32
    gram_block = sum(
        dot(lax.dynamic_slice_in_dim(part, gram_rows, 32, 1), part, (0, 0), HIGHEST)
        for part in (left_own, left_other)
    )
    gram_block, left_own, left_other = lax.optimization_barrier((gram_block, left_own, left_other))
    gram_block = jnp.sum(gathered(gram_block, ROW, 8).reshape(8, 32, 512), axis=0)
    gram_half = gathered(gram_block, CHIPS, 8)
    inverse = inverse_factor(in_core_order(gram_half, to_other_core(gram_half), core))

    partial_right = transposed_product(core, mixed_splits, left_own, left_other)
    right_shard = scatter_sum(partial_right, ROW, 8)

    right_own = dot(right_shard, inverse, (1, 1), HIGHEST)
    right_send = right_own.astype(jnp.bfloat16)
    left_send = dot(tile_left_raw, inverse, (1, 1), HIGH).astype(jnp.bfloat16)
    squares = in_two_parts(jnp.sum(right_own * right_own, axis=0))
    rows = gathered(jnp.concatenate([right_send, left_send, squares]), ROW, 8).reshape(8, 272, 512)
    right_factor = rows[:, :128].reshape(1024, 512)
    tile_left = rows[:, 128:256].reshape(1024, 512)
    squares = in_two_parts(jnp.sum(rows[:, 256:].astype(jnp.float32), axis=(0, 1)))

    tile = gathered(jnp.concatenate([to_tile_owner(right_send), squares]), CHIPS, 8).reshape(8, 144, 512)
    left_factor = [dot(part, inverse, (1, 1), HIGH).astype(jnp.bfloat16) for part in (left_own, left_other)]
    outer = dot(in_core_order(*left_factor, core), right_factor, (1, 1))
    mixed = momentum.astype(jnp.float32) + gradient.astype(jnp.float32)
    new_momentum = (mixed - decay_part * outer).astype(jnp.bfloat16)
    tile, new_momentum = lax.optimization_barrier((tile, new_momentum))

    own_squares = jnp.sum(tile[:, 128:].astype(jnp.float32), axis=(0, 1))
    own = tile[:, :128].reshape(1024, 512)
    other = to_other_core(jnp.concatenate([own, in_two_parts(own_squares)]))
    scale = lax.rsqrt(
        (own_squares + jnp.sum(other[1024:].astype(jnp.float32), axis=0)) / DIN + epsilon
    )
    tile_left = (tile_left.astype(jnp.float32) * scale).astype(jnp.bfloat16)
    update = dot(tile_left, in_core_order(own, other[:1024], core), (1, 1))
    new_weight = (weight.astype(jnp.float32) - step_size * update).astype(jnp.bfloat16)
    partial_projected = dot(tokens, new_weight, (1, 1)).astype(jnp.bfloat16)
    partial_projected, scale, right_factor = lax.optimization_barrier(
        (partial_projected, scale, right_factor)
    )
    projected = scatter_sum(partial_projected, ROW, 8).astype(jnp.bfloat16)
    new_basis = right_factor.astype(jnp.float32) * scale
    return (new_momentum, new_basis, new_weight, projected)


def solution(mesh):
    torus = Mesh(mesh.devices.reshape(4, 2, 4, 2, 2), ("row_0", "row_1", "col_0", "col_1", "col_2"))
    placed = (P(ROW, COL), P(ROW, COL), P(COL, None), P(COL, ROW), P(None, ROW))
    return jax.shard_map(
        per_device,
        mesh=torus,
        in_specs=placed,
        out_specs=(P(ROW, COL), P(COL, None), P(COL, ROW), P(ROW, COL)),
        check_vma=False,
    )
```

profile of v0, /device:TPU:2, one launch (start us, length us, event | category | flops | bytes accessed | tf_op | source)
XLA Modules:
  0.0 275.7 jit_solution(1334304624815660827)
XLA Ops:
  0.7 1.6 copy-done
  2.2 9.2 %fusion.1 = f32[2048,512]{1,0:T(8,128)S(1)} fusion(f32[1024,512]{1,0:T(8,128)S(1)} %copy-done, bf16[2048,1024]{1,0:T(8,128)(2,1)} %param.6, bf16[2048,1024]{1,0:T(8,128)(2,1)} %param.5), kind=kOutput, calls=%fused_computation.6 | convolution fusion | flops 6448742400 | bytes 14680064 | tf_op jit(solution)/shard_map/dot_general | solution.py:121
  11.4 2.0 copy-done.8
  13.4 1.5 constant_dynamic-slice_fusion
  14.9 4.4 %collective-permute-done = f32[1024,512]{1,0:T(8,128)S(1)} collective-permute-done((f32[1024,512]{1,0:T(8,128)}, f32[1024,512]{1,0:T(8,128)S(1)}, u32[]{:S(2)}, u32[]{:S(2)}) %collective-permute-start) | collective-permute-done | bytes 2097184 | tf_op jit(solution)/shard_map/ppermute | solution.py:139
  19.3 3.4 %dynamic-slice_add_fusion = f32[1024,512]{1,0:T(8,128)} fusion(f32[1024,512]{1,0:T(8,128)S(1)} %collective-permute-done, f32[2048,512]{1,0:T(8,128)} %copy-done.8, s32[]{:T(128)S(6)} %select_n.50), kind=kLoop, calls=%fused_computation.25 | loop fusion | flops 524288 | bytes 6291460 | tf_op jit(solution)/shard_map/add | solution.py:220
  22.7 7.8 %all-to-all-start = ((f32[8,128,512]{2,1,0:T(8,128)}), f32[8,128,512]{2,1,0:T(8,128)S(1)}, u32[]{:S(2)}, u32[]{:S(2)}) async-start(f32[8,128,512]{2,1,0:T(8,128)} %bitcast.1), calls=%async_computation | async-start | bytes 4194304 | tf_op jit(solution)/shard_map/all_to_all | solution.py:128
  30.5 6.4 %copy.19 = bf16[2048,1024]{0,1:T(8,128)(2,1)} copy(bf16[2048,1024]{1,0:T(8,128)(2,1)} %param.6) | data formatting | bytes 8388608 | tf_op jit(solution)/shard_map/optimization_barrier | solution.py:221
  36.9 6.4 %copy.18 = bf16[2048,1024]{0,1:T(8,128)(2,1)} copy(bf16[2048,1024]{1,0:T(8,128)(2,1)} %param.5) | data formatting | bytes 8388608 | tf_op jit(solution)/shard_map/optimization_barrier | solution.py:221
  43.3 7.9 %bitcast_convert_fusion.first_ref = bf16[1024,2048]{1,0:T(8,128)(2,1)} fusion(bf16[2048,1024]{0,1:T(8,128)(2,1)} %copy.19, bf16[2048,1024]{0,1:T(8,128)(2,1)} %copy.18), kind=kLoop, calls=%fused_computation.1 | loop fusion | flops 8388608 | bytes 12582912 | tf_op jit(solution)/shard_map/convert_element_type | solution.py:162
  51.2 4.1 %fusion.second_ref = bf16[1024,2048]{1,0:T(8,128)(2,1)} fusion(bf16[2048,1024]{0,1:T(8,128)(2,1)S(1)} %copy-done.5, bf16[2048,1024]{0,1:T(8,128)(2,1)S(1)} %copy-done.7), kind=kLoop, calls=%fused_computation.2 | loop fusion | flops 14680064 | bytes 12582912 | tf_op jit(solution)/shard_map/convert_element_type | solution.py:163
  55.2 7.0 %all-to-all-done = f32[8,128,512]{2,1,0:T(8,128)S(1)} async-done(((f32[8,128,512]{2,1,0:T(8,128)}), f32[8,128,512]{2,1,0:T(8,128)S(1)}, u32[]{:S(2)}, u32[]{:S(2)}) %all-to-all-start) | async-done | bytes 2097184 | tf_op jit(solution)/shard_map/all_to_all | solution.py:128
  62.2 0.2 reduce_sum.75
  62.4 0.3 broadcast_in_dim.84
  62.7 30.4 %all_to_all.40 = f32[8,128,512]{2,1,0:T(8,128)S(1)} all-to-all(f32[8,128,512]{2,1,0:T(8,128)S(1)} %broadcast_in_dim.84), channel_id=1, replica_groups=mesh['row_0'=4,'row_1'=2,'col_0'=4,'col_1'=2,'col_2'=2] {'col_0','col_1'}, dimensions={0} | all-to-all | bytes 4194304 | tf_op jit(solution)/shard_map/all_to_all | solution.py:132
  93.1 1.4 fusion.22
  94.5 2.9 %collective-permute-done.1.other_ref = f32[1024,512]{1,0:T(8,128)} collective-permute-done((f32[1024,512]{1,0:T(8,128)S(1)}, f32[1024,512]{1,0:T(8,128)}, u32[]{:S(2)}, u32[]{:S(2)}) %collective-permute-start.1) | collective-permute-done | bytes 2097184 | tf_op jit(solution)/shard_map/ppermute | solution.py:139
  97.4 3.2 %convolution_add_fusion = f32[32,512]{1,0:T(8,128)S(1)} fusion(f32[32,512]{1,0:T(8,128)S(1)} %fusion.22, f32[1024,512]{1,0:T(8,128)} %collective-permute-done.1.other_ref, s32[]{:T(128)S(6)} %select_n.52), kind=kOutput, calls=%fused_computation.33 | convolution fusion | flops 201342976 | bytes 2752516 | tf_op jit(solution)/shard_map/dot_general | solution.py:121
  100.6 13.4 %all_to_all.41 = f32[8,32,512]{2,1,0:T(8,128)S(1)} all-to-all(f32[8,32,512]{2,1,0:T(8,128)S(1)} %broadcast_in_dim.85), channel_id=1, replica_groups=mesh['row_0'=4,'row_1'=2,'col_0'=4,'col_1'=2,'col_2'=2] {'row_0','row_1'}, dimensions={0} | all-to-all | bytes 1048576 | tf_op jit(solution)/shard_map/all_to_all | solution.py:132
  114.0 0.9 broadcast_in_dim.86
  114.9 3.7 %all-to-all-start.4 = ((f32[8,32,512]{2,1,0:T(8,128)}), f32[8,32,512]{2,1,0:T(8,128)S(1)}, u32[]{:S(2)}, u32[]{:S(2)}) async-start(f32[8,32,512]{2,1,0:T(8,128)} %broadcast_in_dim.86), calls=%async_computation.4 | async-start | bytes 1048576 | tf_op jit(solution)/shard_map/all_to_all | solution.py:132
  118.6 2.2 copy-done.2
  120.8 2.2 copy-done.3
  123.0 12.1 %shard_map.84 = f32[1024,512]{1,0:T(8,128)S(1)} custom-call(s32[1]{0:T(128)} %bitcast.core_ref, bf16[1024,2048]{1,0:T(8,128)(2,1)S(1)} %copy-done.2, bf16[1024,2048]{1,0:T(8,128)(2,1)S(1)} %copy-done.3, f32[1024,512]{1,0:T(8,128)S(1)} %bitcast.35, f32[1024,512]{1,0:T(8,128)} %collective-permute-done.1.other_ref), custom_call_target="tpu_custom_call" | custom-call | tf_op jit(solution)/shard_map/pallas_call | solution.py:191
  135.1 1.3 copy-done.4
  136.4 5.9 %all-to-all-start.2 = ((f32[8,128,512]{2,1,0:T(8,128)}), f32[8,128,512]{2,1,0:T(8,128)}, u32[]{:S(2)}, u32[]{:S(2)}) async-start(f32[8,128,512]{2,1,0:T(8,128)} %bitcast.37), calls=%async_computation.2 | async-start | bytes 4194304 | tf_op jit(solution)/shard_map/all_to_all | solution.py:128
  142.3 3.6 %collective-permute-start.4 = (f32[128,512]{1,0:T(8,128)S(1)}, f32[128,512]{1,0:T(8,128)}, u32[]{:S(2)}, u32[]{:S(2)}) collective-permute-start(f32[128,512]{1,0:T(8,128)S(1)} %reduce_sum.75), channel_id=1, source_target_pairs={{0,0},{1,1},{2,16},{3,17},{4,32},{5,33},{6,48},{7,49},{8,64},{9,65... | collective-permute-start | bytes 786440 | tf_op jit(solution)/shard_map/ppermute | solution.py:150
  146.0 0.1 maximum_select_fusion.4.g_ref
  146.1 23.0 %shard_map.85 = f32[512,512]{1,0:T(8,128)S(1)} custom-call(f32[512,512]{1,0:T(8,128)S(1)} %maximum_select_fusion.4.g_ref), custom_call_target="tpu_custom_call" | custom-call | tf_op jit(solution)/shard_map/pallas_call | solution.py:108
  169.1 5.6 %collective-permute-done.4 = f32[128,512]{1,0:T(8,128)} collective-permute-done((f32[128,512]{1,0:T(8,128)S(1)}, f32[128,512]{1,0:T(8,128)}, u32[]{:S(2)}, u32[]{:S(2)}) %collective-permute-start.4) | collective-permute-done | bytes 262176 | tf_op jit(solution)/shard_map/ppermute | solution.py:150
  174.7 2.3 convolution_convert_fusion.3
  177.0 1.8 reduce_sum.76
  178.8 1.2 fusion.29
  180.0 0.1 select_select_fusion.2
  180.1 0.9 pad_maximum_fusion.1
  181.0 1.5 broadcast_in_dim.90
  182.5 9.5 %all-to-all-start.5 = ((bf16[8,272,512]{2,1,0:T(8,128)(2,1)}), bf16[8,272,512]{2,1,0:T(8,128)(2,1)}, u32[]{:S(2)}, u32[]{:S(2)}) async-start(bf16[8,272,512]{2,1,0:T(8,128)(2,1)} %broadcast_in_dim.90), calls=%async_computation.5 | async-start | bytes 4456448 | tf_op jit(solution)/shard_map/all_to_all | solution.py:132
  192.1 4.4 %convolution_convert_fusion = bf16[1024,512]{1,0:T(8,128)(2,1)} fusion(f32[1024,512]{1,0:T(8,128)} %collective-permute-done.1.other_ref, f32[512,512]{1,0:T(8,128)S(1)} %shard_map.85), kind=kOutput, calls=%fused_computation.28 | convolution fusion | flops 1611137024 | bytes 4194304 | tf_op jit(solution)/shard_map/dot_general | solution.py:121
  196.5 2.8 %convolution_convert_fusion.1 = bf16[1024,512]{1,0:T(8,128)(2,1)} fusion(f32[1024,512]{1,0:T(8,128)S(1)} %bitcast.36, f32[512,512]{1,0:T(8,128)S(1)} %shard_map.85), kind=kOutput, calls=%fused_computation.29 | convolution fusion | flops 1611137024 | bytes 4194304 | tf_op jit(solution)/shard_map/dot_general | solution.py:121
  199.3 3.8 %collective-permute-start.3 = (bf16[128,512]{1,0:T(8,128)(2,1)S(1)}, bf16[128,512]{1,0:T(8,128)(2,1)S(1)}, u32[]{:S(2)}, u32[]{:S(2)}) collective-permute-start(bf16[128,512]{1,0:T(8,128)(2,1)S(1)} %get-tuple-element.52), channel_id=1, source_target_pairs={{0,0},{1,1},{2,16},{3,17},{4,32},{5,33},{6,48},{7,49},{8,64},{9,65... | collective-permute-start | bytes 393224 | tf_op jit(solution)/shard_map/ppermute | solution.py:150
  203.2 13.2 %all-to-all-done.5 = bf16[8,272,512]{2,1,0:T(8,128)(2,1)} async-done(((bf16[8,272,512]{2,1,0:T(8,128)(2,1)}), bf16[8,272,512]{2,1,0:T(8,128)(2,1)}, u32[]{:S(2)}, u32[]{:S(2)}) %all-to-all-start.5) | async-done | bytes 2228256 | tf_op jit(solution)/shard_map/all_to_all | solution.py:132
  216.3 0.9 convert_reduce_fusion.1
  217.3 0.1 select_select_fusion.1
  217.4 3.9 %collective-permute-done.3 = bf16[128,512]{1,0:T(8,128)(2,1)S(1)} collective-permute-done((bf16[128,512]{1,0:T(8,128)(2,1)S(1)}, bf16[128,512]{1,0:T(8,128)(2,1)S(1)}, u32[]{:S(2)}, u32[]{:S(2)}) %collective-permute-start.3) | collective-permute-done | bytes 131104 | tf_op jit(solution)/shard_map/ppermute | solution.py:150
  221.3 1.1 broadcast_in_dim.93
  222.4 9.4 %all-to-all-start.6 = ((bf16[8,144,512]{2,1,0:T(8,128)(2,1)}), bf16[8,144,512]{2,1,0:T(8,128)(2,1)S(1)}, u32[]{:S(2)}, u32[]{:S(2)}) async-start(bf16[8,144,512]{2,1,0:T(8,128)(2,1)} %broadcast_in_dim.93), calls=%async_computation.6 | async-start | bytes 2359296 | tf_op jit(solution)/shard_map/all_to_all | solution.py:132
  231.8 2.9 %fusion.28 = (bf16[8,128,512]{2,1,0:T(8,128)(2,1)}, bf16[8,128,512]{2,1,0:T(8,128)(2,1)S(1)}) fusion(bf16[8,272,512]{2,1,0:T(8,128)(2,1)} %all-to-all-done.5), kind=kLoop, calls=%fused_computation.60 | loop fusion | bytes 4194304 | tf_op jit(solution)/shard_map/slice | solution.py:249
  234.7 8.0 %subtract_convert_fusion.1 = bf16[2048,1024]{0,1:T(8,128)(2,1)} fusion(bf16[2048,1024]{0,1:T(8,128)(2,1)S(1)} %copy-done.6, bf16[2048,1024]{0,1:T(8,128)(2,1)} %copy.18, bf16[1024,512]{1,0:T(8,128)(2,1)S(1)} %bitcast.40, bf16[1024,512]{1,0:T(8,128)(2,1)} %convolution_convert_fusion, bf16[1024,512]{1,0:T(8,128)(2,1)} %convolution_convert_fusion.1, pred[]{:T(512)S(6)} %eq.25), kind=kOutput, calls=%fused_computation.4 | convolution fusion | flops 2169503744 | bytes 15728641 | tf_op jit(solution)/shard_map/dot_general | solution.py:121
  242.7 5.0 %all-to-all-done.6 = bf16[8,144,512]{2,1,0:T(8,128)(2,1)S(1)} async-done(((bf16[8,144,512]{2,1,0:T(8,128)(2,1)}), bf16[8,144,512]{2,1,0:T(8,128)(2,1)S(1)}, u32[]{:S(2)}, u32[]{:S(2)}) %all-to-all-start.6) | async-done | bytes 1179680 | tf_op jit(solution)/shard_map/all_to_all | solution.py:132
  247.7 0.1 slice.25
  247.8 0.1 select_select_fusion
  247.9 0.1 pad_maximum_fusion
  248.0 0.1 collective-permute-start.5
  248.1 2.7 collective-permute-done.5
  250.8 0.1 slice.32
  250.9 4.3 %subtract_convert_fusion = bf16[1024,2048]{1,0:T(8,128)(2,1)S(1)} fusion(bf16[1024,2048]{1,0:T(8,128)(2,1)S(1)} %copy-done.10, bf16[1024,512]{1,0:T(8,128)(2,1)S(1)} %slice.32, bf16[1024,512]{1,0:T(8,128)(2,1)S(1)} %bitcast.39, pred[]{:T(512)S(6)} %eq.25, bf16[1024,512]{1,0:T(8,128)(2,1)S(1)} %bitcast.44, f32[512]{0:T(512)S(1)} %add_rsqrt_fusion), kind=kOutput, calls=%fused_computation.3 | convolution fusion | flops 2166882304 | bytes 11536385 | tf_op jit(solution)/shard_map/dot_general | solution.py:121
  255.2 2.0 copy-done.12
  257.2 1.3 fusion.18
  258.5 1.0 copy.21
  259.5 6.0 %all-to-all-start.7 = ((bf16[8,32,1024]{2,1,0:T(8,128)(2,1)}), bf16[8,32,1024]{2,1,0:T(8,128)(2,1)}, u32[]{:S(2)}, u32[]{:S(2)}) async-start(bf16[8,32,1024]{2,1,0:T(8,128)(2,1)} %bitcast.10), calls=%async_computation.7 | async-start | bytes 1048576 | tf_op jit(solution)/shard_map/all_to_all | solution.py:128
  265.5 6.5 %copy.22 = bf16[2048,1024]{1,0:T(8,128)(2,1)} copy(bf16[2048,1024]{0,1:T(8,128)(2,1)} %subtract_convert_fusion.1) | data formatting | bytes 8388608
  272.1 1.6 convert_multiply_fusion.1
  273.7 0.3 all-to-all-done.7
  273.9 1.8 reduce_sum.82
  (36 shorter events, 0.3 us)
Async XLA Ops:
  0.6 1.6 copy-start
  11.4 2.0 copy-start.8
  14.9 4.4 %collective-permute-start = (f32[1024,512]{1,0:T(8,128)}, f32[1024,512]{1,0:T(8,128)S(1)}, u32[]{:S(2)}, u32[]{:S(2)}) collective-permute-start(f32[1024,512]{1,0:T(8,128)} %constant_dynamic-slice_fusion), channel_id=1, source_target_pairs={{0,1},{1,0},{2,3},{3,2},{4,5},{5,4},{6,7},{7,6},{8,9},{9,8},{10,11... | collective-permute-start | bytes 6291464 | tf_op jit(solution)/shard_map/ppermute | solution.py:139
  22.7 39.5 %all-to-all-start = ((f32[8,128,512]{2,1,0:T(8,128)}), f32[8,128,512]{2,1,0:T(8,128)S(1)}, u32[]{:S(2)}, u32[]{:S(2)}) async-start(f32[8,128,512]{2,1,0:T(8,128)} %bitcast.1), calls=%async_computation | async-start | bytes 4194304 | tf_op jit(solution)/shard_map/all_to_all | solution.py:128
  43.3 7.9 %copy-start.5 = (bf16[2048,1024]{0,1:T(8,128)(2,1)S(1)}, bf16[2048,1024]{0,1:T(8,128)(2,1)}, u32[]{:S(2)}) copy-start(bf16[2048,1024]{0,1:T(8,128)(2,1)} %copy.19) | copy-start | bytes 12582916
  43.3 7.9 %copy-start.7 = (bf16[2048,1024]{0,1:T(8,128)(2,1)S(1)}, bf16[2048,1024]{0,1:T(8,128)(2,1)}, u32[]{:S(2)}) copy-start(bf16[2048,1024]{0,1:T(8,128)(2,1)} %copy.18) | copy-start | bytes 12582916
  93.1 4.3 %collective-permute-start.1 = (f32[1024,512]{1,0:T(8,128)S(1)}, f32[1024,512]{1,0:T(8,128)}, u32[]{:S(2)}, u32[]{:S(2)}) collective-permute-start(f32[1024,512]{1,0:T(8,128)S(1)} %bitcast.33), channel_id=1, source_target_pairs={{0,1},{1,0},{2,3},{3,2},{4,5},{5,4},{6,7},{7,6},{8,9},{9,8},{10,11... | collective-permute-start | bytes 6291464 | tf_op jit(solution)/shard_map/ppermute | solution.py:139
  114.9 21.5 %all-to-all-start.4 = ((f32[8,32,512]{2,1,0:T(8,128)}), f32[8,32,512]{2,1,0:T(8,128)S(1)}, u32[]{:S(2)}, u32[]{:S(2)}) async-start(f32[8,32,512]{2,1,0:T(8,128)} %broadcast_in_dim.86), calls=%async_computation.4 | async-start | bytes 1048576 | tf_op jit(solution)/shard_map/all_to_all | solution.py:132
  118.6 2.2 copy-start.2
  120.8 2.2 copy-start.3
  135.1 1.3 copy-start.4
  136.4 40.6 %all-to-all-start.2 = ((f32[8,128,512]{2,1,0:T(8,128)}), f32[8,128,512]{2,1,0:T(8,128)}, u32[]{:S(2)}, u32[]{:S(2)}) async-start(f32[8,128,512]{2,1,0:T(8,128)} %bitcast.37), calls=%async_computation.2 | async-start | bytes 4194304 | tf_op jit(solution)/shard_map/all_to_all | solution.py:128
  142.3 3.6 %collective-permute-start.2 = (f32[256,512]{1,0:T(8,128)S(1)}, f32[256,512]{1,0:T(8,128)S(1)}, u32[]{:S(2)}, u32[]{:S(2)}) collective-permute-start(f32[256,512]{1,0:T(8,128)S(1)} %bitcast.42), channel_id=1, source_target_pairs={{0,1},{1,0},{2,3},{3,2},{4,5},{5,4},{6,7},{7,6},{8,9},{9,8},{10,11... | collective-permute-start | bytes 1572872 | tf_op jit(solution)/shard_map/ppermute | solution.py:139
  142.3 32.4 %collective-permute-start.4 = (f32[128,512]{1,0:T(8,128)S(1)}, f32[128,512]{1,0:T(8,128)}, u32[]{:S(2)}, u32[]{:S(2)}) collective-permute-start(f32[128,512]{1,0:T(8,128)S(1)} %reduce_sum.75), channel_id=1, source_target_pairs={{0,0},{1,1},{2,16},{3,17},{4,32},{5,33},{6,48},{7,49},{8,64},{9,65... | collective-permute-start | bytes 786440 | tf_op jit(solution)/shard_map/ppermute | solution.py:150
  182.5 33.8 %all-to-all-start.5 = ((bf16[8,272,512]{2,1,0:T(8,128)(2,1)}), bf16[8,272,512]{2,1,0:T(8,128)(2,1)}, u32[]{:S(2)}, u32[]{:S(2)}) async-start(bf16[8,272,512]{2,1,0:T(8,128)(2,1)} %broadcast_in_dim.90), calls=%async_computation.5 | async-start | bytes 4456448 | tf_op jit(solution)/shard_map/all_to_all | solution.py:132
  199.3 21.9 %collective-permute-start.3 = (bf16[128,512]{1,0:T(8,128)(2,1)S(1)}, bf16[128,512]{1,0:T(8,128)(2,1)S(1)}, u32[]{:S(2)}, u32[]{:S(2)}) collective-permute-start(bf16[128,512]{1,0:T(8,128)(2,1)S(1)} %get-tuple-element.52), channel_id=1, source_target_pairs={{0,0},{1,1},{2,16},{3,17},{4,32},{5,33},{6,48},{7,49},{8,64},{9,65... | collective-permute-start | bytes 393224 | tf_op jit(solution)/shard_map/ppermute | solution.py:150
  222.4 25.3 %all-to-all-start.6 = ((bf16[8,144,512]{2,1,0:T(8,128)(2,1)}), bf16[8,144,512]{2,1,0:T(8,128)(2,1)S(1)}, u32[]{:S(2)}, u32[]{:S(2)}) async-start(bf16[8,144,512]{2,1,0:T(8,128)(2,1)} %broadcast_in_dim.93), calls=%async_computation.6 | async-start | bytes 2359296 | tf_op jit(solution)/shard_map/all_to_all | solution.py:132
  231.8 2.9 %copy-start.6 = (bf16[2048,1024]{0,1:T(8,128)(2,1)S(1)}, bf16[2048,1024]{0,1:T(8,128)(2,1)}, u32[]{:S(2)}) copy-start(bf16[2048,1024]{0,1:T(8,128)(2,1)} %copy.19) | copy-start | bytes 12582916
  247.7 3.1 %copy-start.10 = (bf16[1024,2048]{1,0:T(8,128)(2,1)S(1)}, bf16[1024,2048]{1,0:T(8,128)(2,1)}, u32[]{:S(2)}) copy-start(bf16[1024,2048]{1,0:T(8,128)(2,1)} %param.8) | copy-start | bytes 12582916
  247.8 3.1 %copy-start.9 = (bf16[8,128,512]{2,1,0:T(8,128)(2,1)S(1)}, bf16[8,128,512]{2,1,0:T(8,128)(2,1)}, u32[]{:S(2)}) copy-start(bf16[8,128,512]{2,1,0:T(8,128)(2,1)} %get-tuple-element.50) | copy-start | bytes 3145732
  248.0 2.8 %collective-permute-start.5 = (bf16[1040,512]{1,0:T(8,128)(2,1)S(1)}, bf16[1040,512]{1,0:T(8,128)(2,1)S(1)}, u32[]{:S(2)}, u32[]{:S(2)}) collective-permute-start(bf16[1040,512]{1,0:T(8,128)(2,1)S(1)} %pad_maximum_fusion), channel_id=1, source_target_pairs={{0,1},{1,0},{2,3},{3,2},{4,5},{5,4},{6,7},{7,6},{8,9},{9,8},{10,11... | collective-permute-start | bytes 3194888 | tf_op jit(solution)/shard_map/ppermute | solution.py:139
  250.9 6.4 %copy-start.11 = (bf16[256,2048]{1,0:T(8,128)(2,1)S(1)}, bf16[256,2048]{1,0:T(8,128)(2,1)}, u32[]{:S(2)}) copy-start(bf16[256,2048]{1,0:T(8,128)(2,1)} %param.9) | copy-start | bytes 3145732
  255.2 2.0 copy-start.12
  259.5 14.4 %all-to-all-start.7 = ((bf16[8,32,1024]{2,1,0:T(8,128)(2,1)}), bf16[8,32,1024]{2,1,0:T(8,128)(2,1)}, u32[]{:S(2)}, u32[]{:S(2)}) async-start(bf16[8,32,1024]{2,1,0:T(8,128)(2,1)} %bitcast.10), calls=%async_computation.7 | async-start | bytes 1048576 | tf_op jit(solution)/shard_map/all_to_all | solution.py:128
  265.5 10.2 %copy-start.1 = (f32[1024,512]{1,0:T(8,128)S(1)}, f32[1024,512]{1,0:T(8,128)}, u32[]{:S(2)}) copy-start(f32[1024,512]{1,0:T(8,128)} %param.7) | copy-start | bytes 6291460
where the time goes:
time: 278 us; the launch traced here: 276 us
  starting transfers between devices  49.8 us (18%)
  waiting for transfers between devices  44.9 us (16%)
  blocking collectives  43.8 us (16%)
  local copies, waits for them, and re-layouts  40 us (14%)
  matrix products  38 us (14%)
  Pallas kernels  35.1 us (13%)
  other arithmetic  23.1 us (8%)
    all_to_all x2, blocking collectives, gathered(): lax.all_to_all(jnp.broadcast_to(array[None], (length, *array.shape)), axe...  43.8 us
    dot_general x10, matrix products, dot(): lax.dot_general(lhs, rhs, ((dims[:1], dims[1:]), ((), ())), precision=pre...  38 us
    pallas_call x1, Pallas kernels, inverse_factor(): pl.pallas_call(factor_kernel, out_shape=jax.ShapeDtypeStruct((512, 512),...  23 us
    all_to_all x3, starting transfers between devices, gathered(): lax.all_to_all(jnp.broadcast_to(array[None], (length, *array.shape)), axe...  22.6 us
    all_to_all x3, starting transfers between devices, scatter_sum(): lax.all_to_all(pieces, axes, 0, 0, tiled=True).astype(jnp.float32)  19.7 us
    all_to_all x3, waiting for transfers between devices, gathered(): lax.all_to_all(jnp.broadcast_to(array[None], (length, *array.shape)), axe...  18.2 us
    unnamed x27, local copies, waits for them, and re-layouts  17.9 us
    optimization_barrier x2, local copies, waits for them, and re-layouts, per_device(): lax.optimization_barrier((partial_left, momentum, gradient))  12.9 us
  transfers between devices with their start and end apart: 12, of which 9 were waited for; matrix products, arithmetic and copies ran while one was open for 20% of the time, Pallas kernels for 13%

commit v1 on v0

--- a/solution.py
+++ b/solution.py
@@ -163,9 +163,48 @@
     return first, (array - first.astype(jnp.float32)).astype(jnp.bfloat16)
 
 
+def in_hbm(array):
+    return pltpu.with_memory_space_constraint(array, pltpu.HBM)
+
+
+def left_kernel(which_ref, momentum_ref, gradient_ref, right_ref, out_ref, high_ref, low_ref):
+    @pl.when(pl.program_id(0) == 0)
+    def _():
+        right = right_ref[...]
+        high = right.astype(jnp.bfloat16)
+        high_ref[...] = high
+        low_ref[...] = (right - high.astype(jnp.float32)).astype(jnp.bfloat16)
+
+    mixed = momentum_ref[...].astype(jnp.float32) + gradient_ref[...].astype(jnp.float32)
+    first = mixed.astype(jnp.bfloat16)
+    second = (mixed - first.astype(jnp.float32)).astype(jnp.bfloat16)
+    part = jnp.dot(first, high_ref[...], preferred_element_type=jnp.float32)
+    part += jnp.dot(first, low_ref[...], preferred_element_type=jnp.float32)
+    part += jnp.dot(second, high_ref[...], preferred_element_type=jnp.float32)
+    out_ref[...] = part
+
+
+def half_product(which, momentum, gradient, right):
+    rows = pl.BlockSpec((256, 1024), lambda step, which_ref: (which_ref[0] * 4 + step, 0))
+    return pl.pallas_call(
+        left_kernel,
+        out_shape=jax.ShapeDtypeStruct((1024, 512), jnp.float32),
+        grid_spec=pltpu.PrefetchScalarGridSpec(
+            num_scalar_prefetch=1,
+            grid=(4,),
+            in_specs=[rows, rows, pl.BlockSpec((1024, 512), lambda step, which_ref: (0, 0))],
+            out_specs=pl.BlockSpec((256, 512), lambda step, which_ref: (step, 0)),
+            scratch_shapes=[pltpu.VMEM((1024, 512), jnp.bfloat16)] * 2,
+        ),
+        compiler_params=pltpu.CompilerParams(
+            dimension_semantics=("arbitrary",), vmem_limit_bytes=24 * 1024 * 1024
+        ),
+    )(which[None], *(in_hbm(array) for array in (momentum, gradient, right)))
+
+
 def project_kernel(core_ref, first_ref, second_ref, own_ref, other_ref, out_ref):
     step = pl.program_id(0)
-    left = jnp.where(step < 4, own_ref[...], other_ref[...])
+    left = jnp.where(step < 2, own_ref[...], other_ref[...])
     high = left.astype(jnp.bfloat16)
     low = (left - high.astype(jnp.float32)).astype(jnp.bfloat16)
     first = first_ref[...]
@@ -184,43 +223,88 @@
 
 def transposed_product(core, splits, own, other):
     def column(step, core_ref):
-        half = lax.rem(core_ref[0] + step // 4, 2)
-        return 0, half * 4 + lax.rem(step, 4)
-
-    spec = pl.BlockSpec((1024, 256), column)
+        half = lax.rem(core_ref[0] + step // 2, 2)
+        return 0, half * 2 + lax.rem(step, 2)
+
+    spec = pl.BlockSpec((1024, 512), column)
     return pl.pallas_call(
         project_kernel,
         out_shape=jax.ShapeDtypeStruct((1024, 512), jnp.float32),
         grid_spec=pltpu.PrefetchScalarGridSpec(
             num_scalar_prefetch=1,
-            grid=(8,),
+            grid=(4,),
             in_specs=[
                 spec,
                 spec,
-                pl.BlockSpec((256, 512), lambda step, core_ref: (jnp.minimum(step, 3), 0)),
-                pl.BlockSpec((256, 512), lambda step, core_ref: (jnp.maximum(step - 4, 0), 0)),
+                pl.BlockSpec((512, 512), lambda step, core_ref: (jnp.minimum(step, 1), 0)),
+                pl.BlockSpec((512, 512), lambda step, core_ref: (jnp.maximum(step - 2, 0), 0)),
             ],
             out_specs=pl.BlockSpec((1024, 512), lambda step, core_ref: (0, 0)),
         ),
         compiler_params=pltpu.CompilerParams(
+            dimension_semantics=("arbitrary",), vmem_limit_bytes=32 * 1024 * 1024
+        ),
+    )(core[None], *(in_hbm(array) for array in splits), own, other)
+
+
+def send_kernel(pieces_ref, left_ref, inverse_ref, right_ref, out_ref, held_ref):
+    @pl.when(pl.program_id(0) == 0)
+    def _():
+        contract = (((1,), (1,)), ((), ()))
+        total = pieces_ref[0]
+        for i in range(1, 8):
+            total = total + pieces_ref[i]
+        right = lax.dot_general(
+            total, inverse_ref[...], contract, precision=HIGHEST, preferred_element_type=jnp.float32
+        )
+        left = lax.dot_general(
+            left_ref[...], inverse_ref[...], contract, precision=HIGHEST, preferred_element_type=jnp.float32
+        )
+        squares = jnp.sum(right * right, axis=0, keepdims=True)
+        first = squares.astype(jnp.bfloat16).astype(jnp.float32)
+        index = lax.broadcasted_iota(jnp.int32, (16, 512), 0)
+        parts = jnp.where(index == 0, first, jnp.where(index == 1, squares - first, 0.0))
+        right_ref[...] = right.astype(jnp.bfloat16)
+        held_ref[0:128, :] = right.astype(jnp.bfloat16)
+        held_ref[128:256, :] = left.astype(jnp.bfloat16)
+        held_ref[256:272, :] = parts.astype(jnp.bfloat16)
+
+    out_ref[0] = held_ref[...]
+
+
+def right_and_left_to_send(pieces, left, inverse):
+    return pl.pallas_call(
+        send_kernel,
+        out_shape=(
+            jax.ShapeDtypeStruct((128, 512), jnp.bfloat16),
+            jax.ShapeDtypeStruct((8, 272, 512), jnp.bfloat16),
+        ),
+        grid=(8,),
+        in_specs=[
+            pl.BlockSpec((8, 128, 512), lambda copy: (0, 0, 0)),
+            pl.BlockSpec((128, 512), lambda copy: (0, 0)),
+            pl.BlockSpec((512, 512), lambda copy: (0, 0)),
+        ],
+        out_specs=(
+            pl.BlockSpec((128, 512), lambda copy: (0, 0)),
+            pl.BlockSpec((1, 272, 512), lambda copy: (copy, 0, 0)),
+        ),
+        scratch_shapes=[pltpu.VMEM((272, 512), jnp.bfloat16)],
+        compiler_params=pltpu.CompilerParams(
             dimension_semantics=("arbitrary",), vmem_limit_bytes=24 * 1024 * 1024
         ),
-    )(core[None], *splits, own, other)
+    )(pieces, left, inverse)
 
 
 def per_device(momentum, gradient, right_prev, weight, tokens):
     core = lax.axis_index(CORE)
     chip = lax.axis_index(CHIPS)
 
-    def half(array, which):
-        return lax.dynamic_slice_in_dim(array, which * 1024, 1024, 0)
-
-    mixed = momentum.astype(jnp.float32) + gradient.astype(jnp.float32)
-    partial_left = dot(mixed, right_prev, (1, 0), HIGH)
-    partial_left = half(partial_left, core) + to_other_core(half(partial_left, 1 - core))
-    partial_left, momentum, gradient = lax.optimization_barrier((partial_left, momentum, gradient))
+    partial_other = to_other_core(half_product(1 - core, momentum, gradient, right_prev))
+    partial_left = half_product(core, momentum, gradient, right_prev) + partial_other
+    partial_left, late_momentum, late_gradient = lax.optimization_barrier((partial_left, momentum, gradient))
     left_shard = scatter_sum(partial_left, CHIPS, 8)
-    mixed_splits = split((momentum.astype(jnp.float32) + gradient.astype(jnp.float32)).T)
+    mixed_splits = split((late_momentum.astype(jnp.float32) + late_gradient.astype(jnp.float32)).T)
     left_shard, mixed_splits = lax.optimization_barrier((left_shard, mixed_splits))
 
     left_own = gathered(left_shard, CHIPS, 8)
@@ -234,24 +318,24 @@
     )
     gram_block, left_own, left_other = lax.optimization_barrier((gram_block, left_own, left_other))
     gram_block = jnp.sum(gathered(gram_block, ROW, 8).reshape(8, 32, 512), axis=0)
+    partial_right = transposed_product(core, mixed_splits, left_own, left_other)
+    gram_block, partial_right = lax.optimization_barrier((gram_block, partial_right))
     gram_half = gathered(gram_block, CHIPS, 8)
     inverse = inverse_factor(in_core_order(gram_half, to_other_core(gram_half), core))
 
-    partial_right = transposed_product(core, mixed_splits, left_own, left_other)
-    right_shard = scatter_sum(partial_right, ROW, 8)
-
-    right_own = dot(right_shard, inverse, (1, 1), HIGHEST)
-    right_send = right_own.astype(jnp.bfloat16)
-    left_send = dot(tile_left_raw, inverse, (1, 1), HIGH).astype(jnp.bfloat16)
-    squares = in_two_parts(jnp.sum(right_own * right_own, axis=0))
-    rows = gathered(jnp.concatenate([right_send, left_send, squares]), ROW, 8).reshape(8, 272, 512)
+    pieces = lax.all_to_all(partial_right.reshape(8, 128, 512), ROW, 0, 0, tiled=True)
+    right_send, copies = right_and_left_to_send(pieces, tile_left_raw, inverse)
+    rows = lax.all_to_all(copies, ROW, 0, 0, tiled=True)
+    tile_right = to_tile_owner(right_send)
+    left_factor = [dot(part, inverse, (1, 1), HIGH).astype(jnp.bfloat16) for part in (left_own, left_other)]
+    left_factor = in_core_order(*left_factor, core)
+    rows, tile_right = lax.optimization_barrier((rows, tile_right))
     right_factor = rows[:, :128].reshape(1024, 512)
     tile_left = rows[:, 128:256].reshape(1024, 512)
     squares = in_two_parts(jnp.sum(rows[:, 256:].astype(jnp.float32), axis=(0, 1)))
 
-    tile = gathered(jnp.concatenate([to_tile_owner(right_send), squares]), CHIPS, 8).reshape(8, 144, 512)
-    left_factor = [dot(part, inverse, (1, 1), HIGH).astype(jnp.bfloat16) for part in (left_own, left_other)]
-    outer = dot(in_core_order(*left_factor, core), right_factor, (1, 1))
+    tile = gathered(jnp.concatenate([tile_right, squares]), CHIPS, 8).reshape(8, 144, 512)
+    outer = dot(left_factor, right_factor, (1, 1))
     mixed = momentum.astype(jnp.float32) + gradient.astype(jnp.float32)
     new_momentum = (mixed - decay_part * outer).astype(jnp.bfloat16)
     tile, new_momentum = lax.optimization_barrier((tile, new_momentum))
@@ -266,9 +350,6 @@
     update = dot(tile_left, in_core_order(own, other[:1024], core), (1, 1))
     new_weight = (weight.astype(jnp.float32) - step_size * update).astype(jnp.bfloat16)
     partial_projected = dot(tokens, new_weight, (1, 1)).astype(jnp.bfloat16)
-    partial_projected, scale, right_factor = lax.optimization_barrier(
-        (partial_projected, scale, right_factor)
-    )
     projected = scatter_sum(partial_projected, ROW, 8).astype(jnp.bfloat16)
     new_basis = right_factor.astype(jnp.float32) * scale
     return (new_momentum, new_basis, new_weight, projected)

time: 278 us -> 264 us (0.950)
  local copies, waits for them, and re-layouts: 40 us -> 23 us
  Pallas kernels: 35.1 us -> 50.2 us
  matrix products: 38 us -> 28.2 us
    pallas_call x0 -> x3, Pallas kernels: none -> 17.1 us  [the longest x2 13 us: half_product(): pl.pallas_call(left_kernel, out_shape=jax.ShapeDtypeStruct((1024, 512), j...]
    all_to_all x0 -> x2, starting transfers between devices: none -> 14.8 us  [the longest x1 9.36 us: per_device(): rows = lax.all_to_all(copies, ROW, 0, 0, tiled=True)]
    all_to_all x3 -> x2, waiting for transfers between devices: 18.2 us -> 4.88 us  [gathered(): lax.all_to_all(jnp.broadcast_to(array[None], (length, *array.shape)), axe...]
    unnamed x27 -> x26, local copies, waits for them, and re-layouts: 17.9 us -> 4.9 us
    dot_general x10 -> x7, matrix products: 38 us -> 28.2 us  [dot(): lax.dot_general(lhs, rhs, ((dims[:1], dims[1:]), ((), ())), precision=pre...]
    ppermute x2, waiting for transfers between devices: 9.54 us -> 18.8 us  [to_tile_owner(): return lax.ppermute(array, ALL, pairs)]
    all_to_all x3 -> x2, starting transfers between devices: 22.6 us -> 14 us  [gathered(): lax.all_to_all(jnp.broadcast_to(array[None], (length, *array.shape)), axe...]
    all_to_all x3 -> x2, waiting for transfers between devices: 7.22 us -> 13.8 us  [scatter_sum(): lax.all_to_all(pieces, axes, 0, 0, tiled=True).astype(jnp.float32)]
  transfers between devices with their start and end apart: 12 -> 12, of which waited for: 9 -> 8; matrix products, arithmetic and copies ran while one was open for 20% -> 19% of each run, Pallas kernels for 13% -> 15%
where the time goes in v1:
time: 264 us; the launch traced here: 262 us
  Pallas kernels  50.2 us (19%)
  starting transfers between devices  49.6 us (19%)
  blocking collectives  46 us (17%)
  waiting for transfers between devices  43.5 us (16%)
  matrix products  28.2 us (11%)
  local copies, waits for them, and re-layouts  23 us (9%)
  other arithmetic  20.6 us (8%)
    all_to_all x2, blocking collectives, gathered(): lax.all_to_all(jnp.broadcast_to(array[None], (length, *array.shape)), axe...  46 us
    dot_general x7, matrix products, dot(): lax.dot_general(lhs, rhs, ((dims[:1], dims[1:]), ((), ())), precision=pre...  28.2 us
    pallas_call x1, Pallas kernels, inverse_factor(): pl.pallas_call(factor_kernel, out_shape=jax.ShapeDtypeStruct((512, 512),...  23 us
    ppermute x2, waiting for transfers between devices, to_tile_owner(): return lax.ppermute(array, ALL, pairs)  18.8 us
    all_to_all x2, starting transfers between devices, scatter_sum(): lax.all_to_all(pieces, axes, 0, 0, tiled=True).astype(jnp.float32)  15.6 us
    all_to_all x2, starting transfers between devices, gathered(): lax.all_to_all(jnp.broadcast_to(array[None], (length, *array.shape)), axe...  14 us
    all_to_all x2, waiting for transfers between devices, scatter_sum(): lax.all_to_all(pieces, axes, 0, 0, tiled=True).astype(jnp.float32)  13.8 us
    pallas_call x2, Pallas kernels, half_product(): pl.pallas_call(left_kernel, out_shape=jax.ShapeDtypeStruct((1024, 512), j...  13 us
  transfers between devices with their start and end apart: 12, of which 8 were waited for; matrix products, arithmetic and copies ran while one was open for 19% of the time, Pallas kernels for 15%

profile of v1, /device:TPU:2, one launch (start us, length us, event | category | flops | bytes accessed | tf_op | source)
XLA Modules:
  0.0 261.9 jit_solution(13206609014272365445)
XLA Ops:
  0.6 0.0 copy-start
  0.7 6.5 %shard_map.85 = f32[1024,512]{1,0:T(8,128)S(1)} custom-call(s32[1]{0:T(128)} %bitcast.1.which_ref, bf16[2048,1024]{1,0:T(8,128)(2,1)} %momentum_ref.3, bf16[2048,1024]{1,0:T(8,128)(2,1)} %gradient_ref.3, f32[1024,512]{1,0:T(8,128)} %right_ref.3), custom_call_target="tpu_custom_call" | custom-call | tf_op jit(solution)/shard_map/pallas_call | solution.py:189
  7.2 0.1 collective-permute-start
  7.3 6.5 %shard_map.84 = f32[1024,512]{1,0:T(8,128)S(1)} custom-call(s32[1]{0:T(128)} %bitcast.which_ref.core_ref, bf16[2048,1024]{1,0:T(8,128)(2,1)} %momentum_ref.3, bf16[2048,1024]{1,0:T(8,128)(2,1)} %gradient_ref.3, f32[1024,512]{1,0:T(8,128)} %right_ref.3), custom_call_target="tpu_custom_call" | custom-call | tf_op jit(solution)/shard_map/pallas_call | solution.py:189
  13.8 0.0 collective-permute-done
  13.8 1.8 add.39
  15.6 7.8 %all-to-all-start = ((f32[8,128,512]{2,1,0:T(8,128)}), f32[8,128,512]{2,1,0:T(8,128)S(1)}, u32[]{:S(2)}, u32[]{:S(2)}) async-start(f32[8,128,512]{2,1,0:T(8,128)} %bitcast.2), calls=%async_computation | async-start | bytes 4194304 | tf_op jit(solution)/shard_map/all_to_all | solution.py:128
  23.3 6.4 %copy.11 = bf16[2048,1024]{0,1:T(8,128)(2,1)} copy(bf16[2048,1024]{1,0:T(8,128)(2,1)} %momentum_ref.3) | data formatting | bytes 8388608 | tf_op jit(solution)/shard_map/optimization_barrier | solution.py:305
  29.8 6.4 %copy.12 = bf16[2048,1024]{0,1:T(8,128)(2,1)} copy(bf16[2048,1024]{1,0:T(8,128)(2,1)} %gradient_ref.3) | data formatting | bytes 8388608 | tf_op jit(solution)/shard_map/optimization_barrier | solution.py:305
  36.2 7.9 %fusion.second_ref = bf16[1024,2048]{1,0:T(8,128)(2,1)} fusion(bf16[2048,1024]{0,1:T(8,128)(2,1)} %copy.12, bf16[2048,1024]{0,1:T(8,128)(2,1)} %copy.11), kind=kLoop, calls=%fused_computation.2 | loop fusion | flops 14680064 | bytes 12582912 | tf_op jit(solution)/shard_map/convert_element_type | solution.py:163
  44.2 4.0 %bitcast_convert_fusion.first_ref = bf16[1024,2048]{1,0:T(8,128)(2,1)} fusion(bf16[2048,1024]{0,1:T(8,128)(2,1)S(1)} %copy-done.7, bf16[2048,1024]{0,1:T(8,128)(2,1)S(1)} %copy-done.6), kind=kLoop, calls=%fused_computation.1 | loop fusion | flops 8388608 | bytes 12582912 | tf_op jit(solution)/shard_map/convert_element_type | solution.py:162
  48.2 7.2 %all-to-all-done = f32[8,128,512]{2,1,0:T(8,128)S(1)} async-done(((f32[8,128,512]{2,1,0:T(8,128)}), f32[8,128,512]{2,1,0:T(8,128)S(1)}, u32[]{:S(2)}, u32[]{:S(2)}) %all-to-all-start) | async-done | bytes 2097184 | tf_op jit(solution)/shard_map/all_to_all | solution.py:128
  55.4 0.2 reduce_sum.57
  55.6 0.3 broadcast_in_dim.70
  55.9 31.4 %all_to_all.40 = f32[8,128,512]{2,1,0:T(8,128)S(1)} all-to-all(f32[8,128,512]{2,1,0:T(8,128)S(1)} %broadcast_in_dim.70), channel_id=1, replica_groups=mesh['row_0'=4,'row_1'=2,'col_0'=4,'col_1'=2,'col_2'=2] {'col_0','col_1'}, dimensions={0} | all-to-all | bytes 4194304 | tf_op jit(solution)/shard_map/all_to_all | solution.py:132
  87.3 0.0 collective-permute-start.1
  87.3 1.4 fusion.17
  88.7 2.9 %collective-permute-done.1.other_ref = f32[1024,512]{1,0:T(8,128)} collective-permute-done((f32[1024,512]{1,0:T(8,128)S(1)}, f32[1024,512]{1,0:T(8,128)}, u32[]{:S(2)}, u32[]{:S(2)}) %collective-permute-start.1) | collective-permute-done | bytes 2097184 | tf_op jit(solution)/shard_map/ppermute | solution.py:139
  91.6 3.2 %convolution_add_fusion = f32[32,512]{1,0:T(8,128)S(1)} fusion(f32[32,512]{1,0:T(8,128)S(1)} %fusion.17, f32[1024,512]{1,0:T(8,128)} %collective-permute-done.1.other_ref, s32[]{:T(128)S(6)} %select_n.38), kind=kOutput, calls=%fused_computation.26 | convolution fusion | flops 201342976 | bytes 2752516 | tf_op jit(solution)/shard_map/dot_general | solution.py:121
  94.7 0.9 broadcast_in_dim.71
  95.6 5.3 %all-to-all-start.2 = ((f32[8,32,512]{2,1,0:T(8,128)}), f32[8,32,512]{2,1,0:T(8,128)}, u32[]{:S(2)}, u32[]{:S(2)}) async-start(f32[8,32,512]{2,1,0:T(8,128)} %broadcast_in_dim.71), calls=%async_computation.2 | async-start | bytes 1048576 | tf_op jit(solution)/shard_map/all_to_all | solution.py:132
  100.9 10.1 %shard_map.86 = f32[1024,512]{1,0:T(8,128)S(1)} custom-call(s32[1]{0:T(128)} %bitcast.which_ref.core_ref, bf16[1024,2048]{1,0:T(8,128)(2,1)} %bitcast_convert_fusion.first_ref, bf16[1024,2048]{1,0:T(8,128)(2,1)} %fusion.second_ref, f32[1024,512]{1,0:T(8,128)S(1)} %bitcast.32, f32[1024,512]{1,0:T(8,128)} %collective-permute-done.1.other_ref), custom_call_target="tpu_custom_call" | custom-call | tf_op jit(solution)/shard_map/pallas_call | solution.py:230
  111.0 0.0 copy-start.4
  111.0 1.3 copy-done.4
  112.3 1.1 reduce_sum.58
  113.4 0.1 broadcast_in_dim.72
  113.4 14.6 %all_to_all.41 = f32[8,32,512]{2,1,0:T(8,128)} all-to-all(f32[8,32,512]{2,1,0:T(8,128)S(1)} %broadcast_in_dim.72), channel_id=1, replica_groups=mesh['row_0'=4,'row_1'=2,'col_0'=4,'col_1'=2,'col_2'=2] {'col_0','col_1'}, dimensions={0} | all-to-all | bytes 1048576 | tf_op jit(solution)/shard_map/all_to_all | solution.py:132
  128.0 5.5 %all-to-all-start.3 = ((f32[8,128,512]{2,1,0:T(8,128)}), f32[8,128,512]{2,1,0:T(8,128)}, u32[]{:S(2)}, u32[]{:S(2)}) async-start(f32[8,128,512]{2,1,0:T(8,128)} %bitcast.34), calls=%async_computation.3 | async-start | bytes 4194304 | tf_op jit(solution)/shard_map/all_to_all | solution.py:326
  133.5 1.9 collective-permute-start.2
  135.4 0.3 collective-permute-done.3
  135.7 1.9 maximum_select_fusion.4.g_ref
  137.6 23.0 %shard_map.87.inverse_ref = f32[512,512]{1,0:T(8,128)S(1)} custom-call(f32[512,512]{1,0:T(8,128)S(1)} %maximum_select_fusion.4.g_ref), custom_call_target="tpu_custom_call" | custom-call | tf_op jit(solution)/shard_map/pallas_call | solution.py:108
  160.6 0.0 copy-start.1
  160.6 1.0 copy-done.1
  161.6 2.0 collective-permute-done.2.left_ref
  163.5 1.2 copy-done.2
  164.8 4.1 %shard_map.88 = (bf16[128,512]{1,0:T(8,128)(2,1)S(1)}, bf16[8,272,512]{2,1,0:T(8,128)(2,1)S(1)}) custom-call(f32[8,128,512]{2,1,0:T(8,128)} %all-to-all-done.3.pieces_ref, f32[128,512]{1,0:T(8,128)S(1)} %collective-permute-done.2.left_ref, f32[512,512]{1,0:T(8,128)S(1)} %copy-done.2), custom_call_target="tpu_custom_call" | custom-call | tf_op jit(solution)/shard_map/pallas_call | solution.py:276
  168.9 0.0 copy-start.5
  168.9 1.4 copy-done.5
  170.2 9.4 %all-to-all-start.5 = ((bf16[8,272,512]{2,1,0:T(8,128)(2,1)}), bf16[8,272,512]{2,1,0:T(8,128)(2,1)}, u32[]{:S(2)}, u32[]{:S(2)}) async-start(bf16[8,272,512]{2,1,0:T(8,128)(2,1)} %copy-done.5), calls=%async_computation.5 | async-start | bytes 4456448 | tf_op jit(solution)/shard_map/all_to_all | solution.py:328
  179.6 4.1 %convolution_convert_fusion.1 = bf16[1024,512]{1,0:T(8,128)(2,1)} fusion(f32[1024,512]{1,0:T(8,128)S(1)} %bitcast.33, f32[512,512]{1,0:T(8,128)} %copy-done.1), kind=kOutput, calls=%fused_computation.24 | convolution fusion | flops 1611137024 | bytes 4194304 | tf_op jit(solution)/shard_map/dot_general | solution.py:121
  183.7 3.1 %collective-permute-start.4 = (bf16[128,512]{1,0:T(8,128)(2,1)S(1)}, bf16[128,512]{1,0:T(8,128)(2,1)S(1)}, u32[]{:S(2)}, u32[]{:S(2)}) collective-permute-start(bf16[128,512]{1,0:T(8,128)(2,1)S(1)} %get-tuple-element.33), channel_id=1, source_target_pairs={{0,0},{1,1},{2,16},{3,17},{4,32},{5,33},{6,48},{7,49},{8,64},{9,65... | collective-permute-start | bytes 393224 | tf_op jit(solution)/shard_map/ppermute | solution.py:150
  186.8 4.5 %convolution_convert_fusion = bf16[1024,512]{1,0:T(8,128)(2,1)} fusion(f32[1024,512]{1,0:T(8,128)} %collective-permute-done.1.other_ref, f32[512,512]{1,0:T(8,128)S(1)} %copy-done.3), kind=kOutput, calls=%fused_computation.23 | convolution fusion | flops 1611137024 | bytes 4194304 | tf_op jit(solution)/shard_map/dot_general | solution.py:121
  191.3 16.9 %collective-permute-done.4 = bf16[128,512]{1,0:T(8,128)(2,1)S(1)} collective-permute-done((bf16[128,512]{1,0:T(8,128)(2,1)S(1)}, bf16[128,512]{1,0:T(8,128)(2,1)S(1)}, u32[]{:S(2)}, u32[]{:S(2)}) %collective-permute-start.4) | collective-permute-done | bytes 131104 | tf_op jit(solution)/shard_map/ppermute | solution.py:150
  208.2 0.9 convert_reduce_fusion.1
  209.1 0.1 select_select_fusion.1
  209.2 1.1 broadcast_in_dim.76
  210.3 8.7 %all-to-all-start.6 = ((bf16[8,144,512]{2,1,0:T(8,128)(2,1)}), bf16[8,144,512]{2,1,0:T(8,128)(2,1)S(1)}, u32[]{:S(2)}, u32[]{:S(2)}) async-start(bf16[8,144,512]{2,1,0:T(8,128)(2,1)} %broadcast_in_dim.76), calls=%async_computation.6 | async-start | bytes 2359296 | tf_op jit(solution)/shard_map/all_to_all | solution.py:132
  219.1 2.9 %fusion.23 = (bf16[8,128,512]{2,1,0:T(8,128)(2,1)}, bf16[8,128,512]{2,1,0:T(8,128)(2,1)S(1)}) fusion(bf16[8,272,512]{2,1,0:T(8,128)(2,1)} %all-to-all-done.5), kind=kLoop, calls=%fused_computation.48 | loop fusion | bytes 4194304 | tf_op jit(solution)/shard_map/slice | solution.py:334
  221.9 8.6 %subtract_convert_fusion.1 = bf16[2048,1024]{1,0:T(8,128)(2,1)} fusion(bf16[2048,1024]{1,0:T(8,128)(2,1)S(1)} %copy-done.8, bf16[2048,1024]{1,0:T(8,128)(2,1)} %momentum_ref.3, bf16[1024,512]{1,0:T(8,128)(2,1)S(1)} %bitcast.37, bf16[1024,512]{1,0:T(8,128)(2,1)} %convolution_convert_fusion, bf16[1024,512]{1,0:T(8,128)(2,1)} %convolution_convert_fusion.1, ...), kind=kOutput, calls=%fused_computation.4 | convolution fusion | flops 2169503744 | bytes 15728641 | tf_op jit(solution)/shard_map/dot_general | solution.py:121
  230.5 4.9 %all-to-all-done.6 = bf16[8,144,512]{2,1,0:T(8,128)(2,1)S(1)} async-done(((bf16[8,144,512]{2,1,0:T(8,128)(2,1)}), bf16[8,144,512]{2,1,0:T(8,128)(2,1)S(1)}, u32[]{:S(2)}, u32[]{:S(2)}) %all-to-all-start.6) | async-done | bytes 1179680 | tf_op jit(solution)/shard_map/all_to_all | solution.py:132
  235.4 0.1 slice.24
  235.5 0.1 select_select_fusion
  235.6 0.1 pad_maximum_fusion
  235.7 0.1 collective-permute-start.5
  235.8 2.7 %collective-permute-done.5 = bf16[1040,512]{1,0:T(8,128)(2,1)S(1)} collective-permute-done((bf16[1040,512]{1,0:T(8,128)(2,1)S(1)}, bf16[1040,512]{1,0:T(8,128)(2,1)S(1)}, u32[]{:S(2)}, u32[]{:S(2)}) %collective-permute-start.5) | collective-permute-done | bytes 1064992 | tf_op jit(solution)/shard_map/ppermute | solution.py:139
  238.5 0.1 slice.29
  238.6 4.3 %subtract_convert_fusion = bf16[1024,2048]{1,0:T(8,128)(2,1)S(1)} fusion(bf16[1024,2048]{1,0:T(8,128)(2,1)S(1)} %copy-done.11, bf16[1024,512]{1,0:T(8,128)(2,1)S(1)} %slice.29, bf16[1024,512]{1,0:T(8,128)(2,1)S(1)} %bitcast.36, pred[]{:T(512)S(6)} %eq.19, bf16[1024,512]{1,0:T(8,128)(2,1)S(1)} %bitcast.40, f32[512]{0:T(512)S(1)} %add_rsqrt_fusion), kind=kOutput, calls=%fused_computation.3 | convolution fusion | flops 2166882304 | bytes 11536385 | tf_op jit(solution)/shard_map/dot_general | solution.py:121
  242.9 0.0 copy-start.12
  242.9 2.2 convolution_convert_fusion.2
  245.1 7.8 %all-to-all-start.7 = ((bf16[8,32,1024]{2,1,0:T(8,128)(2,1)}), bf16[8,32,1024]{2,1,0:T(8,128)(2,1)S(1)}, u32[]{:S(2)}, u32[]{:S(2)}) async-start(bf16[8,32,1024]{2,1,0:T(8,128)(2,1)} %bitcast.11), calls=%async_computation.7 | async-start | bytes 1048576 | tf_op jit(solution)/shard_map/all_to_all | solution.py:128
  252.9 1.7 convert_multiply_fusion.1
  254.6 6.6 %all-to-all-done.7 = bf16[8,32,1024]{2,1,0:T(8,128)(2,1)S(1)} async-done(((bf16[8,32,1024]{2,1,0:T(8,128)(2,1)}), bf16[8,32,1024]{2,1,0:T(8,128)(2,1)S(1)}, u32[]{:S(2)}, u32[]{:S(2)}) %all-to-all-start.7) | async-done | bytes 524320 | tf_op jit(solution)/shard_map/all_to_all | solution.py:128
  261.2 0.7 reduce_sum.62
  (28 shorter events, 0.1 us)
Async XLA Ops:
  0.6 242.3 %copy-start = (bf16[256,2048]{1,0:T(8,128)(2,1)S(1)}, bf16[256,2048]{1,0:T(8,128)(2,1)}, u32[]{:S(2)}) copy-start(bf16[256,2048]{1,0:T(8,128)(2,1)} %param.9) | copy-start | bytes 3145732
  7.2 6.6 %collective-permute-start = (f32[1024,512]{1,0:T(8,128)S(1)}, f32[1024,512]{1,0:T(8,128)S(1)}, u32[]{:S(2)}, u32[]{:S(2)}) collective-permute-start(f32[1024,512]{1,0:T(8,128)S(1)} %shard_map.85), channel_id=1, source_target_pairs={{0,1},{1,0},{2,3},{3,2},{4,5},{5,4},{6,7},{7,6},{8,9},{9,8},{10,11... | collective-permute-start | bytes 6291464 | tf_op jit(solution)/shard_map/ppermute | solution.py:139
  15.6 39.8 %all-to-all-start = ((f32[8,128,512]{2,1,0:T(8,128)}), f32[8,128,512]{2,1,0:T(8,128)S(1)}, u32[]{:S(2)}, u32[]{:S(2)}) async-start(f32[8,128,512]{2,1,0:T(8,128)} %bitcast.2), calls=%async_computation | async-start | bytes 4194304 | tf_op jit(solution)/shard_map/all_to_all | solution.py:128
  36.2 7.9 %copy-start.6 = (bf16[2048,1024]{0,1:T(8,128)(2,1)S(1)}, bf16[2048,1024]{0,1:T(8,128)(2,1)}, u32[]{:S(2)}) copy-start(bf16[2048,1024]{0,1:T(8,128)(2,1)} %copy.11) | copy-start | bytes 12582916
  36.2 8.0 %copy-start.7 = (bf16[2048,1024]{0,1:T(8,128)(2,1)S(1)}, bf16[2048,1024]{0,1:T(8,128)(2,1)}, u32[]{:S(2)}) copy-start(bf16[2048,1024]{0,1:T(8,128)(2,1)} %copy.12) | copy-start | bytes 12582916
  55.6 31.7 %copy-start.9 = (f32[128,512]{1,0:T(8,128)}, f32[128,512]{1,0:T(8,128)S(1)}, u32[]{:S(2)}) copy-start(f32[128,512]{1,0:T(8,128)S(1)} %reduce_sum.57) | copy-start | bytes 786436
  87.3 4.3 %collective-permute-start.1 = (f32[1024,512]{1,0:T(8,128)S(1)}, f32[1024,512]{1,0:T(8,128)}, u32[]{:S(2)}, u32[]{:S(2)}) collective-permute-start(f32[1024,512]{1,0:T(8,128)S(1)} %bitcast.30), channel_id=1, source_target_pairs={{0,1},{1,0},{2,3},{3,2},{4,5},{5,4},{6,7},{7,6},{8,9},{9,8},{10,11... | collective-permute-start | bytes 6291464 | tf_op jit(solution)/shard_map/ppermute | solution.py:139
  95.6 16.7 %all-to-all-start.2 = ((f32[8,32,512]{2,1,0:T(8,128)}), f32[8,32,512]{2,1,0:T(8,128)}, u32[]{:S(2)}, u32[]{:S(2)}) async-start(f32[8,32,512]{2,1,0:T(8,128)} %broadcast_in_dim.71), calls=%async_computation.2 | async-start | bytes 1048576 | tf_op jit(solution)/shard_map/all_to_all | solution.py:132
  111.0 1.3 copy-start.4
  128.0 35.5 %all-to-all-start.3 = ((f32[8,128,512]{2,1,0:T(8,128)}), f32[8,128,512]{2,1,0:T(8,128)}, u32[]{:S(2)}, u32[]{:S(2)}) async-start(f32[8,128,512]{2,1,0:T(8,128)} %bitcast.34), calls=%async_computation.3 | async-start | bytes 4194304 | tf_op jit(solution)/shard_map/all_to_all | solution.py:326
  133.5 2.3 collective-permute-start.3
  133.5 30.1 %collective-permute-start.2 = (f32[128,512]{1,0:T(8,128)}, f32[128,512]{1,0:T(8,128)S(1)}, u32[]{:S(2)}, u32[]{:S(2)}) collective-permute-start(f32[128,512]{1,0:T(8,128)} %copy-done.9), channel_id=1, source_target_pairs={{0,0},{1,1},{2,16},{3,17},{4,32},{5,33},{6,48},{7,49},{8,64},{9,65... | collective-permute-start | bytes 786440 | tf_op jit(solution)/shard_map/ppermute | solution.py:150
  160.6 1.0 copy-start.1
  163.5 1.2 copy-start.2
  168.9 1.4 copy-start.5
  170.2 37.9 %all-to-all-start.5 = ((bf16[8,272,512]{2,1,0:T(8,128)(2,1)}), bf16[8,272,512]{2,1,0:T(8,128)(2,1)}, u32[]{:S(2)}, u32[]{:S(2)}) async-start(bf16[8,272,512]{2,1,0:T(8,128)(2,1)} %copy-done.5), calls=%async_computation.5 | async-start | bytes 4456448 | tf_op jit(solution)/shard_map/all_to_all | solution.py:328
  179.6 7.2 %copy-start.3 = (f32[512,512]{1,0:T(8,128)S(1)}, f32[512,512]{1,0:T(8,128)}, u32[]{:S(2)}) copy-start(f32[512,512]{1,0:T(8,128)} %copy-done.1) | copy-start | bytes 3145732
  183.7 24.4 %collective-permute-start.4 = (bf16[128,512]{1,0:T(8,128)(2,1)S(1)}, bf16[128,512]{1,0:T(8,128)(2,1)S(1)}, u32[]{:S(2)}, u32[]{:S(2)}) collective-permute-start(bf16[128,512]{1,0:T(8,128)(2,1)S(1)} %get-tuple-element.33), channel_id=1, source_target_pairs={{0,0},{1,1},{2,16},{3,17},{4,32},{5,33},{6,48},{7,49},{8,64},{9,65... | collective-permute-start | bytes 393224 | tf_op jit(solution)/shard_map/ppermute | solution.py:150
  210.3 25.1 %all-to-all-start.6 = ((bf16[8,144,512]{2,1,0:T(8,128)(2,1)}), bf16[8,144,512]{2,1,0:T(8,128)(2,1)S(1)}, u32[]{:S(2)}, u32[]{:S(2)}) async-start(bf16[8,144,512]{2,1,0:T(8,128)(2,1)} %broadcast_in_dim.76), calls=%async_computation.6 | async-start | bytes 2359296 | tf_op jit(solution)/shard_map/all_to_all | solution.py:132
  219.1 2.9 %copy-start.8 = (bf16[2048,1024]{1,0:T(8,128)(2,1)S(1)}, bf16[2048,1024]{1,0:T(8,128)(2,1)}, u32[]{:S(2)}) copy-start(bf16[2048,1024]{1,0:T(8,128)(2,1)} %gradient_ref.3) | copy-start | bytes 12582916
  235.4 3.2 %copy-start.11 = (bf16[1024,2048]{1,0:T(8,128)(2,1)S(1)}, bf16[1024,2048]{1,0:T(8,128)(2,1)}, u32[]{:S(2)}) copy-start(bf16[1024,2048]{1,0:T(8,128)(2,1)} %param.8) | copy-start | bytes 12582916
  235.6 3.0 %copy-start.10 = (bf16[8,128,512]{2,1,0:T(8,128)(2,1)S(1)}, bf16[8,128,512]{2,1,0:T(8,128)(2,1)}, u32[]{:S(2)}) copy-start(bf16[8,128,512]{2,1,0:T(8,128)(2,1)} %get-tuple-element.42) | copy-start | bytes 3145732
  235.7 2.8 %collective-permute-start.5 = (bf16[1040,512]{1,0:T(8,128)(2,1)S(1)}, bf16[1040,512]{1,0:T(8,128)(2,1)S(1)}, u32[]{:S(2)}, u32[]{:S(2)}) collective-permute-start(bf16[1040,512]{1,0:T(8,128)(2,1)S(1)} %pad_maximum_fusion), channel_id=1, source_target_pairs={{0,1},{1,0},{2,3},{3,2},{4,5},{5,4},{6,7},{7,6},{8,9},{9,8},{10,11... | collective-permute-start | bytes 3194888 | tf_op jit(solution)/shard_map/ppermute | solution.py:139
  242.9 2.2 copy-start.12
  245.1 16.1 %all-to-all-start.7 = ((bf16[8,32,1024]{2,1,0:T(8,128)(2,1)}), bf16[8,32,1024]{2,1,0:T(8,128)(2,1)S(1)}, u32[]{:S(2)}, u32[]{:S(2)}) async-start(bf16[8,32,1024]{2,1,0:T(8,128)(2,1)} %bitcast.11), calls=%async_computation.7 | async-start | bytes 1048576 | tf_op jit(solution)/shard_map/all_to_all | solution.py:128

commit v2 on v1

--- a/solution.py
+++ b/solution.py
@@ -79,8 +79,10 @@
                     total = total - columns[q, i] * solved[t][i]
                 rows[q][t] = total
 
-def factor_kernel(g_ref, x_ref, z_ref, d_ref, u_ref):
-    z_ref[...] = g_ref[...]
+def factor_kernel(core_ref, own_ref, other_ref, x_ref, z_ref, d_ref, u_ref):
+    start = pl.multiple_of(core_ref[0] * 256, 256)
+    z_ref[pl.ds(start, 256), :] = own_ref[...]
+    z_ref[pl.ds(pl.multiple_of(256 - start, 256), 256), :] = other_ref[...]
     def step(k, carry):
         at = pl.multiple_of(k * 128, 128)
         places = [pl.multiple_of(lax.rem(k + t, 4) * 128, 128) for t in range(4)]
@@ -104,17 +106,24 @@
     lax.fori_loop(0, 4, step, 0)
 
 
-def inverse_factor(gram):
+def inverse_factor(core, own, other):
+    half = pl.BlockSpec((256, 512), lambda step, core_ref: (0, 0))
     return pl.pallas_call(
         factor_kernel,
         out_shape=jax.ShapeDtypeStruct((512, 512), jnp.float32),
-        scratch_shapes=[
-            pltpu.VMEM((512, 512), jnp.float32),
-            pltpu.VMEM((4, 128, 128), jnp.float32),
-            pltpu.VMEM((4, 128, 128), jnp.float32),
-        ],
+        grid_spec=pltpu.PrefetchScalarGridSpec(
+            num_scalar_prefetch=1,
+            grid=(1,),
+            in_specs=[half, half],
+            out_specs=pl.BlockSpec((512, 512), lambda step, core_ref: (0, 0)),
+            scratch_shapes=[
+                pltpu.VMEM((512, 512), jnp.float32),
+                pltpu.VMEM((4, 128, 128), jnp.float32),
+                pltpu.VMEM((4, 128, 128), jnp.float32),
+            ],
+        ),
         compiler_params=pltpu.CompilerParams(vmem_limit_bytes=16 * 1024 * 1024),
-    )(gram)
+    )(core[None], own, other)
 
 
 def dot(lhs, rhs, dims, precision=None):
@@ -158,30 +167,25 @@
     return jnp.where(index == 0, first[None], jnp.where(index == 1, second[None], zero))
 
 
-def split(array):
-    first = array.astype(jnp.bfloat16)
-    return first, (array - first.astype(jnp.float32)).astype(jnp.bfloat16)
-
-
 def in_hbm(array):
     return pltpu.with_memory_space_constraint(array, pltpu.HBM)
 
 
-def left_kernel(which_ref, momentum_ref, gradient_ref, right_ref, out_ref, high_ref, low_ref):
+def left_kernel(which_ref, momentum_ref, gradient_ref, right_ref, out_ref, parts_ref):
     @pl.when(pl.program_id(0) == 0)
     def _():
         right = right_ref[...]
         high = right.astype(jnp.bfloat16)
-        high_ref[...] = high
-        low_ref[...] = (right - high.astype(jnp.float32)).astype(jnp.bfloat16)
+        parts_ref[0:1024, :] = high
+        parts_ref[1024:2048, :] = (right - high.astype(jnp.float32)).astype(jnp.bfloat16)
+        parts_ref[2048:3072, :] = high
 
     mixed = momentum_ref[...].astype(jnp.float32) + gradient_ref[...].astype(jnp.float32)
     first = mixed.astype(jnp.bfloat16)
     second = (mixed - first.astype(jnp.float32)).astype(jnp.bfloat16)
-    part = jnp.dot(first, high_ref[...], preferred_element_type=jnp.float32)
-    part += jnp.dot(first, low_ref[...], preferred_element_type=jnp.float32)
-    part += jnp.dot(second, high_ref[...], preferred_element_type=jnp.float32)
-    out_ref[...] = part
+    out_ref[...] = jnp.dot(
+        jnp.concatenate([first, first, second], axis=1), parts_ref[...], preferred_element_type=jnp.float32
+    )
 
 
 def half_product(which, momentum, gradient, right):
@@ -194,7 +198,7 @@
             grid=(4,),
             in_specs=[rows, rows, pl.BlockSpec((1024, 512), lambda step, which_ref: (0, 0))],
             out_specs=pl.BlockSpec((256, 512), lambda step, which_ref: (step, 0)),
-            scratch_shapes=[pltpu.VMEM((1024, 512), jnp.bfloat16)] * 2,
+            scratch_shapes=[pltpu.VMEM((3072, 512), jnp.bfloat16)],
         ),
         compiler_params=pltpu.CompilerParams(
             dimension_semantics=("arbitrary",), vmem_limit_bytes=24 * 1024 * 1024
@@ -202,15 +206,20 @@
     )(which[None], *(in_hbm(array) for array in (momentum, gradient, right)))
 
 
-def project_kernel(core_ref, first_ref, second_ref, own_ref, other_ref, out_ref):
+def project_kernel(core_ref, momentum_ref, gradient_ref, own_ref, other_ref, out_ref):
     step = pl.program_id(0)
-    left = jnp.where(step < 2, own_ref[...], other_ref[...])
+    left = jnp.where(step < 4, own_ref[...], other_ref[...])
     high = left.astype(jnp.bfloat16)
     low = (left - high.astype(jnp.float32)).astype(jnp.bfloat16)
-    first = first_ref[...]
-    part = jnp.dot(first, high, preferred_element_type=jnp.float32)
-    part += jnp.dot(first, low, preferred_element_type=jnp.float32)
-    part += jnp.dot(second_ref[...], high, preferred_element_type=jnp.float32)
+    mixed = momentum_ref[...].astype(jnp.float32) + gradient_ref[...].astype(jnp.float32)
+    first = mixed.astype(jnp.bfloat16)
+    second = (mixed - first.astype(jnp.float32)).astype(jnp.bfloat16)
+    part = lax.dot_general(
+        jnp.concatenate([first, first, second], axis=0),
+        jnp.concatenate([high, low, high], axis=0),
+        (((0,), (0,)), ((), ())),
+        preferred_element_type=jnp.float32,
+    )
 
     @pl.when(step == 0)
     def _():
@@ -221,30 +230,30 @@
         out_ref[...] += part
 
 
-def transposed_product(core, splits, own, other):
-    def column(step, core_ref):
-        half = lax.rem(core_ref[0] + step // 2, 2)
-        return 0, half * 2 + lax.rem(step, 2)
-
-    spec = pl.BlockSpec((1024, 512), column)
+def transposed_product(core, momentum, gradient, own, other):
+    def rows(step, core_ref):
+        half = lax.rem(core_ref[0] + step // 4, 2)
+        return half * 4 + lax.rem(step, 4), 0
+
+    spec = pl.BlockSpec((256, 1024), rows)
     return pl.pallas_call(
         project_kernel,
-        out_shape=jax.ShapeDtypeStruct((1024, 512), jnp.float32),
+        out_shape=pltpu.HBM((1024, 512), jnp.float32),
         grid_spec=pltpu.PrefetchScalarGridSpec(
             num_scalar_prefetch=1,
-            grid=(4,),
+            grid=(8,),
             in_specs=[
                 spec,
                 spec,
-                pl.BlockSpec((512, 512), lambda step, core_ref: (jnp.minimum(step, 1), 0)),
-                pl.BlockSpec((512, 512), lambda step, core_ref: (jnp.maximum(step - 2, 0), 0)),
+                pl.BlockSpec((256, 512), lambda step, core_ref: (jnp.minimum(step, 3), 0)),
+                pl.BlockSpec((256, 512), lambda step, core_ref: (jnp.maximum(step - 4, 0), 0)),
             ],
             out_specs=pl.BlockSpec((1024, 512), lambda step, core_ref: (0, 0)),
         ),
         compiler_params=pltpu.CompilerParams(
             dimension_semantics=("arbitrary",), vmem_limit_bytes=32 * 1024 * 1024
         ),
-    )(core[None], *(in_hbm(array) for array in splits), own, other)
+    )(core[None], *(in_hbm(array) for array in (momentum, gradient)), own, other)
 
 
 def send_kernel(pieces_ref, left_ref, inverse_ref, right_ref, out_ref, held_ref):
@@ -302,26 +311,22 @@
 
     partial_other = to_other_core(half_product(1 - core, momentum, gradient, right_prev))
     partial_left = half_product(core, momentum, gradient, right_prev) + partial_other
-    partial_left, late_momentum, late_gradient = lax.optimization_barrier((partial_left, momentum, gradient))
     left_shard = scatter_sum(partial_left, CHIPS, 8)
-    mixed_splits = split((late_momentum.astype(jnp.float32) + late_gradient.astype(jnp.float32)).T)
-    left_shard, mixed_splits = lax.optimization_barrier((left_shard, mixed_splits))
-
     left_own = gathered(left_shard, CHIPS, 8)
     left_other = to_other_core(left_own)
     tile_left_raw = to_tile_owner(left_shard)
 
     gram_rows = core * 256 + chip * 32
     gram_block = sum(
-        dot(lax.dynamic_slice_in_dim(part, gram_rows, 32, 1), part, (0, 0), HIGHEST)
+        dot(lax.dynamic_slice_in_dim(part, gram_rows, 32, 1), part, (0, 0), HIGH)
         for part in (left_own, left_other)
     )
     gram_block, left_own, left_other = lax.optimization_barrier((gram_block, left_own, left_other))
     gram_block = jnp.sum(gathered(gram_block, ROW, 8).reshape(8, 32, 512), axis=0)
-    partial_right = transposed_product(core, mixed_splits, left_own, left_other)
+    partial_right = transposed_product(core, momentum, gradient, left_own, left_other)
     gram_block, partial_right = lax.optimization_barrier((gram_block, partial_right))
     gram_half = gathered(gram_block, CHIPS, 8)
-    inverse = inverse_factor(in_core_order(gram_half, to_other_core(gram_half), core))
+    inverse = inverse_factor(core, gram_half, to_other_core(gram_half))
 
     pieces = lax.all_to_all(partial_right.reshape(8, 128, 512), ROW, 0, 0, tiled=True)
     right_send, copies = right_and_left_to_send(pieces, tile_left_raw, inverse)

time: 264 us -> 260 us (0.985)
  blocking collectives: 46 us -> 81.4 us
  other arithmetic: 20.6 us -> 5.42 us
  local copies, waits for them, and re-layouts: 23 us -> 9.91 us
  starting transfers between devices: 49.6 us -> 41.8 us
  waiting for transfers between devices: 43.5 us -> 38.5 us
  Pallas kernels: 50.2 us -> 53.4 us
    all_to_all x0 -> x1, blocking collectives: none -> 36.3 us  [scatter_sum(): lax.all_to_all(pieces, axes, 0, 0, tiled=True).astype(jnp.float32)]
    optimization_barrier x2 -> x0, local copies, waits for them, and re-layouts: 12.9 us -> none  [per_device(): lax.optimization_barrier((partial_left, momentum, gradient))]
    convert_element_type x2 -> x0, other arithmetic: 12 us -> none  [the longest x1 7.94 us: split(): return (first, (array - first.astype(jnp.float32)).astype(jnp.bfloat16))]
    all_to_all x2 -> x1, starting transfers between devices: 15.6 us -> 7.81 us  [scatter_sum(): lax.all_to_all(pieces, axes, 0, 0, tiled=True).astype(jnp.float32)]
    all_to_all x2 -> x1, waiting for transfers between devices: 13.8 us -> 6.63 us  [scatter_sum(): lax.all_to_all(pieces, axes, 0, 0, tiled=True).astype(jnp.float32)]
    pallas_call x1, Pallas kernels: 10.1 us -> 13.2 us  [transposed_product(): pl.pallas_call(project_kernel, out_shape=pltpu.HBM((1024, 512), jnp.float...]
  transfers between devices with their start and end apart: 12 -> 11, of which waited for: 8 -> 6; matrix products, arithmetic and copies ran while one was open for 19% -> 8% of each run, Pallas kernels for 15% -> 17%
where the time goes in v2:
time: 260 us; the launch traced here: 258 us
  blocking collectives  81.4 us (31%)
  Pallas kernels  53.4 us (21%)
  starting transfers between devices  41.8 us (16%)
  waiting for transfers between devices  38.5 us (15%)
  matrix products  26.2 us (10%)
  local copies, waits for them, and re-layouts  9.91 us (4%)
  other arithmetic  5.42 us (2%)
    all_to_all x2, blocking collectives, gathered(): lax.all_to_all(jnp.broadcast_to(array[None], (length, *array.shape)), axe...  45.1 us
    all_to_all x1, blocking collectives, scatter_sum(): lax.all_to_all(pieces, axes, 0, 0, tiled=True).astype(jnp.float32)  36.3 us
    dot_general x7, matrix products, dot(): lax.dot_general(lhs, rhs, ((dims[:1], dims[1:]), ((), ())), precision=pre...  26.2 us
    pallas_call x1, Pallas kernels, inverse_factor(): pl.pallas_call(factor_kernel, out_shape=jax.ShapeDtypeStruct((512, 512),...  23 us
    ppermute x2, waiting for transfers between devices, to_tile_owner(): return lax.ppermute(array, ALL, pairs)  21 us
    all_to_all x2, starting transfers between devices, gathered(): lax.all_to_all(jnp.broadcast_to(array[None], (length, *array.shape)), axe...  14.1 us
    pallas_call x1, Pallas kernels, transposed_product(): pl.pallas_call(project_kernel, out_shape=pltpu.HBM((1024, 512), jnp.float...  13.2 us
    pallas_call x2, Pallas kernels, half_product(): pl.pallas_call(left_kernel, out_shape=jax.ShapeDtypeStruct((1024, 512), j...  13.1 us
  transfers between devices with their start and end apart: 11, of which 6 were waited for; matrix products, arithmetic and copies ran while one was open for 8% of the time, Pallas kernels for 17%

profile of v2, /device:TPU:2, one launch (start us, length us, event | category | flops | bytes accessed | tf_op | source)
XLA Modules:
  0.0 257.5 jit_solution(10995250748121152212)
XLA Ops:
  0.6 0.0 copy-start
  0.7 6.6 %shard_map.85 = f32[1024,512]{1,0:T(8,128)S(1)} custom-call(s32[1]{0:T(128)} %bitcast.1.which_ref, bf16[2048,1024]{1,0:T(8,128)(2,1)} %momentum_ref.5, bf16[2048,1024]{1,0:T(8,128)(2,1)} %gradient_ref.5, f32[1024,512]{1,0:T(8,128)} %right_ref.3), custom_call_target="tpu_custom_call" | custom-call | tf_op jit(solution)/shard_map/pallas_call | solution.py:193
  7.2 0.1 collective-permute-start
  7.3 6.5 %shard_map.84 = f32[1024,512]{1,0:T(8,128)S(1)} custom-call(s32[1]{0:T(128)} %bitcast.which_ref.core_ref, bf16[2048,1024]{1,0:T(8,128)(2,1)} %momentum_ref.5, bf16[2048,1024]{1,0:T(8,128)(2,1)} %gradient_ref.5, f32[1024,512]{1,0:T(8,128)} %right_ref.3), custom_call_target="tpu_custom_call" | custom-call | tf_op jit(solution)/shard_map/pallas_call | solution.py:193
  13.8 0.0 collective-permute-done
  13.8 0.5 add.36
  14.3 36.3 %all_to_all.40 = f32[8,128,512]{2,1,0:T(8,128)S(1)} all-to-all(f32[8,128,512]{2,1,0:T(8,128)S(1)} %bitcast.29), channel_id=1, replica_groups=mesh['row_0'=4,'row_1'=2,'col_0'=4,'col_1'=2,'col_2'=2] {'col_0','col_1'}, dimensions={0} | all-to-all | bytes 4194304 | tf_op jit(solution)/shard_map/all_to_all | solution.py:137
  50.6 0.2 reduce_sum.57
  50.9 0.0 copy-start.7
  50.9 0.3 broadcast_in_dim.71
  51.1 30.5 %all_to_all.41 = f32[8,128,512]{2,1,0:T(8,128)S(1)} all-to-all(f32[8,128,512]{2,1,0:T(8,128)S(1)} %broadcast_in_dim.71), channel_id=1, replica_groups=mesh['row_0'=4,'row_1'=2,'col_0'=4,'col_1'=2,'col_2'=2] {'col_0','col_1'}, dimensions={0} | all-to-all | bytes 4194304 | tf_op jit(solution)/shard_map/all_to_all | solution.py:141
  81.6 0.0 copy-done.7
  81.6 0.0 collective-permute-start.1
  81.6 0.9 fusion.16
  82.5 3.4 %collective-permute-done.1.other_ref = f32[1024,512]{1,0:T(8,128)} collective-permute-done((f32[1024,512]{1,0:T(8,128)S(1)}, f32[1024,512]{1,0:T(8,128)}, u32[]{:S(2)}, u32[]{:S(2)}) %collective-permute-start.1) | collective-permute-done | bytes 2097184 | tf_op jit(solution)/shard_map/ppermute | solution.py:148
  85.9 2.6 %convolution_add_fusion = f32[32,512]{1,0:T(8,128)S(1)} fusion(f32[32,512]{1,0:T(8,128)S(1)} %fusion.16, f32[1024,512]{1,0:T(8,128)} %collective-permute-done.1.other_ref, s32[]{:T(128)S(6)} %select_n.30), kind=kOutput, calls=%fused_computation.22 | convolution fusion | flops 100679680 | bytes 2752516 | tf_op jit(solution)/shard_map/dot_general | solution.py:130
  88.6 0.9 broadcast_in_dim.72
  89.4 5.3 %all-to-all-start.2 = ((f32[8,32,512]{2,1,0:T(8,128)}), f32[8,32,512]{2,1,0:T(8,128)}, u32[]{:S(2)}, u32[]{:S(2)}) async-start(f32[8,32,512]{2,1,0:T(8,128)} %broadcast_in_dim.72), calls=%async_computation.2 | async-start | bytes 1048576 | tf_op jit(solution)/shard_map/all_to_all | solution.py:141
  94.7 13.2 %shard_map.86 = f32[1024,512]{1,0:T(8,128)} custom-call(s32[1]{0:T(128)} %bitcast.which_ref.core_ref, bf16[2048,1024]{1,0:T(8,128)(2,1)} %momentum_ref.5, bf16[2048,1024]{1,0:T(8,128)(2,1)} %gradient_ref.5, f32[1024,512]{1,0:T(8,128)S(1)} %bitcast.25, f32[1024,512]{1,0:T(8,128)} %collective-permute-done.1.other_ref), custom_call_target="tpu_custom_call" | custom-call | tf_op jit(solution)/shard_map/pallas_call | solution.py:239
  107.9 0.0 all-to-all-done.2
  107.9 1.1 reduce_sum.58
  109.0 0.1 broadcast_in_dim.73
  109.1 14.6 %all_to_all.42 = f32[8,32,512]{2,1,0:T(8,128)} all-to-all(f32[8,32,512]{2,1,0:T(8,128)S(1)} %broadcast_in_dim.73), channel_id=1, replica_groups=mesh['row_0'=4,'row_1'=2,'col_0'=4,'col_1'=2,'col_2'=2] {'col_0','col_1'}, dimensions={0} | all-to-all | bytes 1048576 | tf_op jit(solution)/shard_map/all_to_all | solution.py:141
  123.7 5.5 %all-to-all-start.3 = ((f32[8,128,512]{2,1,0:T(8,128)}), f32[8,128,512]{2,1,0:T(8,128)}, u32[]{:S(2)}, u32[]{:S(2)}) async-start(f32[8,128,512]{2,1,0:T(8,128)} %bitcast.30), calls=%async_computation.3 | async-start | bytes 4194304 | tf_op jit(solution)/shard_map/all_to_all | solution.py:331
  129.1 0.0 collective-permute-start.3
  129.1 2.1 collective-permute-start.2
  131.2 0.0 collective-permute-done.3.other_ref
  131.3 1.0 copy-done.5
  132.3 23.0 %shard_map.87.inverse_ref = f32[512,512]{1,0:T(8,128)S(1)} custom-call(s32[1]{0:T(128)} %bitcast.which_ref.core_ref, f32[256,512]{1,0:T(8,128)S(1)} %bitcast.28, f32[256,512]{1,0:T(8,128)S(1)} %collective-permute-done.3.other_ref), custom_call_target="tpu_custom_call" | custom-call | tf_op jit(solution)/shard_map/pallas_call | solution.py:111
  155.3 0.0 copy-start.1
  155.3 1.0 copy-done.1
  156.3 2.9 %collective-permute-done.2.left_ref = f32[128,512]{1,0:T(8,128)S(1)} collective-permute-done((f32[128,512]{1,0:T(8,128)}, f32[128,512]{1,0:T(8,128)S(1)}, u32[]{:S(2)}, u32[]{:S(2)}) %collective-permute-start.2) | collective-permute-done | bytes 262176 | tf_op jit(solution)/shard_map/ppermute | solution.py:159
  159.2 0.0 all-to-all-done.3.pieces_ref
  159.2 1.2 copy-done.2
  160.4 4.1 %shard_map.88 = (bf16[128,512]{1,0:T(8,128)(2,1)S(1)}, bf16[8,272,512]{2,1,0:T(8,128)(2,1)S(1)}) custom-call(f32[8,128,512]{2,1,0:T(8,128)} %all-to-all-done.3.pieces_ref, f32[128,512]{1,0:T(8,128)S(1)} %collective-permute-done.2.left_ref, f32[512,512]{1,0:T(8,128)S(1)} %copy-done.2), custom_call_target="tpu_custom_call" | custom-call | tf_op jit(solution)/shard_map/pallas_call | solution.py:285
  164.5 0.0 copy-start.4
  164.5 1.4 copy-done.4
  165.9 9.4 %all-to-all-start.5 = ((bf16[8,272,512]{2,1,0:T(8,128)(2,1)}), bf16[8,272,512]{2,1,0:T(8,128)(2,1)}, u32[]{:S(2)}, u32[]{:S(2)}) async-start(bf16[8,272,512]{2,1,0:T(8,128)(2,1)} %copy-done.4), calls=%async_computation.5 | async-start | bytes 4456448 | tf_op jit(solution)/shard_map/all_to_all | solution.py:333
  175.3 4.8 %convolution_convert_fusion = bf16[1024,512]{1,0:T(8,128)(2,1)} fusion(f32[1024,512]{1,0:T(8,128)} %collective-permute-done.1.other_ref, f32[512,512]{1,0:T(8,128)} %copy-done.1), kind=kOutput, calls=%fused_computation.19 | convolution fusion | flops 1611137024 | bytes 4194304 | tf_op jit(solution)/shard_map/dot_general | solution.py:130
  180.0 2.8 %collective-permute-start.4 = (bf16[128,512]{1,0:T(8,128)(2,1)S(1)}, bf16[128,512]{1,0:T(8,128)(2,1)S(1)}, u32[]{:S(2)}, u32[]{:S(2)}) collective-permute-start(bf16[128,512]{1,0:T(8,128)(2,1)S(1)} %get-tuple-element.21), channel_id=1, source_target_pairs={{0,0},{1,1},{2,16},{3,17},{4,32},{5,33},{6,48},{7,49},{8,64},{9,65... | collective-permute-start | bytes 393224 | tf_op jit(solution)/shard_map/ppermute | solution.py:159
  182.9 0.0 copy-done.3
  182.9 2.8 %convolution_convert_fusion.1 = bf16[1024,512]{1,0:T(8,128)(2,1)} fusion(f32[1024,512]{1,0:T(8,128)S(1)} %bitcast.26, f32[512,512]{1,0:T(8,128)S(1)} %copy-done.3), kind=kOutput, calls=%fused_computation.20 | convolution fusion | flops 1611137024 | bytes 4194304 | tf_op jit(solution)/shard_map/dot_general | solution.py:130
  185.7 18.0 %collective-permute-done.4 = bf16[128,512]{1,0:T(8,128)(2,1)S(1)} collective-permute-done((bf16[128,512]{1,0:T(8,128)(2,1)S(1)}, bf16[128,512]{1,0:T(8,128)(2,1)S(1)}, u32[]{:S(2)}, u32[]{:S(2)}) %collective-permute-start.4) | collective-permute-done | bytes 131104 | tf_op jit(solution)/shard_map/ppermute | solution.py:159
  203.8 0.0 all-to-all-done.5
  203.8 0.9 convert_reduce_fusion.1
  204.7 0.1 select_select_fusion.1
  204.8 1.1 broadcast_in_dim.77
  205.9 8.8 %all-to-all-start.6 = ((bf16[8,144,512]{2,1,0:T(8,128)(2,1)}), bf16[8,144,512]{2,1,0:T(8,128)(2,1)S(1)}, u32[]{:S(2)}, u32[]{:S(2)}) async-start(bf16[8,144,512]{2,1,0:T(8,128)(2,1)} %broadcast_in_dim.77), calls=%async_computation.6 | async-start | bytes 2359296 | tf_op jit(solution)/shard_map/all_to_all | solution.py:141
  214.8 2.9 %fusion.22 = (bf16[8,128,512]{2,1,0:T(8,128)(2,1)}, bf16[8,128,512]{2,1,0:T(8,128)(2,1)S(1)}) fusion(bf16[8,272,512]{2,1,0:T(8,128)(2,1)} %all-to-all-done.5), kind=kLoop, calls=%fused_computation.43 | loop fusion | bytes 4194304 | tf_op jit(solution)/shard_map/slice | solution.py:339
  217.6 8.6 %subtract_convert_fusion.1 = bf16[2048,1024]{1,0:T(8,128)(2,1)} fusion(bf16[2048,1024]{1,0:T(8,128)(2,1)S(1)} %copy-done.6, bf16[2048,1024]{1,0:T(8,128)(2,1)} %momentum_ref.5, bf16[1024,512]{1,0:T(8,128)(2,1)S(1)} %bitcast.33, bf16[1024,512]{1,0:T(8,128)(2,1)} %convolution_convert_fusion, bf16[1024,512]{1,0:T(8,128)(2,1)} %convolution_convert_fusion.1, ...), kind=kOutput, calls=%fused_computation.1 | convolution fusion | flops 2169503744 | bytes 15728641 | tf_op jit(solution)/shard_map/dot_general | solution.py:130
  226.2 4.8 %all-to-all-done.6 = bf16[8,144,512]{2,1,0:T(8,128)(2,1)S(1)} async-done(((bf16[8,144,512]{2,1,0:T(8,128)(2,1)}), bf16[8,144,512]{2,1,0:T(8,128)(2,1)S(1)}, u32[]{:S(2)}, u32[]{:S(2)}) %all-to-all-start.6) | async-done | bytes 1179680 | tf_op jit(solution)/shard_map/all_to_all | solution.py:141
  231.1 0.1 slice.24
  231.2 0.1 select_select_fusion
  231.2 0.1 pad_maximum_fusion
  231.3 0.1 collective-permute-start.5
  231.4 2.7 %collective-permute-done.5 = bf16[1040,512]{1,0:T(8,128)(2,1)S(1)} collective-permute-done((bf16[1040,512]{1,0:T(8,128)(2,1)S(1)}, bf16[1040,512]{1,0:T(8,128)(2,1)S(1)}, u32[]{:S(2)}, u32[]{:S(2)}) %collective-permute-start.5) | collective-permute-done | bytes 1064992 | tf_op jit(solution)/shard_map/ppermute | solution.py:148
  234.1 0.1 slice.29
  234.2 4.3 %subtract_convert_fusion = bf16[1024,2048]{1,0:T(8,128)(2,1)S(1)} fusion(bf16[1024,2048]{1,0:T(8,128)(2,1)S(1)} %copy-done.9, bf16[1024,512]{1,0:T(8,128)(2,1)S(1)} %slice.29, bf16[1024,512]{1,0:T(8,128)(2,1)S(1)} %bitcast.32, pred[]{:T(512)S(6)} %eq.20, bf16[1024,512]{1,0:T(8,128)(2,1)S(1)} %bitcast.34, f32[512]{0:T(512)S(1)} %add_rsqrt_fusion), kind=kOutput, calls=%fused_computation | convolution fusion | flops 2166882304 | bytes 11536385 | tf_op jit(solution)/shard_map/dot_general | solution.py:130
  238.5 0.0 copy-start.10
  238.5 2.2 convolution_convert_fusion.2
  240.7 7.8 %all-to-all-start.7 = ((bf16[8,32,1024]{2,1,0:T(8,128)(2,1)}), bf16[8,32,1024]{2,1,0:T(8,128)(2,1)S(1)}, u32[]{:S(2)}, u32[]{:S(2)}) async-start(bf16[8,32,1024]{2,1,0:T(8,128)(2,1)} %bitcast.10), calls=%async_computation.7 | async-start | bytes 1048576 | tf_op jit(solution)/shard_map/all_to_all | solution.py:137
  248.5 1.7 convert_multiply_fusion.1
  250.2 6.6 %all-to-all-done.7 = bf16[8,32,1024]{2,1,0:T(8,128)(2,1)S(1)} async-done(((bf16[8,32,1024]{2,1,0:T(8,128)(2,1)}), bf16[8,32,1024]{2,1,0:T(8,128)(2,1)S(1)}, u32[]{:S(2)}, u32[]{:S(2)}) %all-to-all-start.7) | async-done | bytes 524320 | tf_op jit(solution)/shard_map/all_to_all | solution.py:137
  256.8 0.7 reduce_sum.62
  (18 shorter events, 0.1 us)
Async XLA Ops:
  0.6 237.9 %copy-start = (bf16[256,2048]{1,0:T(8,128)(2,1)S(1)}, bf16[256,2048]{1,0:T(8,128)(2,1)}, u32[]{:S(2)}) copy-start(bf16[256,2048]{1,0:T(8,128)(2,1)} %param.9) | copy-start | bytes 3145732
  7.2 6.6 %collective-permute-start = (f32[1024,512]{1,0:T(8,128)S(1)}, f32[1024,512]{1,0:T(8,128)S(1)}, u32[]{:S(2)}, u32[]{:S(2)}) collective-permute-start(f32[1024,512]{1,0:T(8,128)S(1)} %shard_map.85), channel_id=1, source_target_pairs={{0,1},{1,0},{2,3},{3,2},{4,5},{5,4},{6,7},{7,6},{8,9},{9,8},{10,11... | collective-permute-start | bytes 6291464 | tf_op jit(solution)/shard_map/ppermute | solution.py:148
  50.9 30.8 %copy-start.7 = (f32[128,512]{1,0:T(8,128)}, f32[128,512]{1,0:T(8,128)S(1)}, u32[]{:S(2)}) copy-start(f32[128,512]{1,0:T(8,128)S(1)} %reduce_sum.57) | copy-start | bytes 786436
  81.6 4.3 %collective-permute-start.1 = (f32[1024,512]{1,0:T(8,128)S(1)}, f32[1024,512]{1,0:T(8,128)}, u32[]{:S(2)}, u32[]{:S(2)}) collective-permute-start(f32[1024,512]{1,0:T(8,128)S(1)} %bitcast.23), channel_id=1, source_target_pairs={{0,1},{1,0},{2,3},{3,2},{4,5},{5,4},{6,7},{7,6},{8,9},{9,8},{10,11... | collective-permute-start | bytes 6291464 | tf_op jit(solution)/shard_map/ppermute | solution.py:148
  89.4 18.5 %all-to-all-start.2 = ((f32[8,32,512]{2,1,0:T(8,128)}), f32[8,32,512]{2,1,0:T(8,128)}, u32[]{:S(2)}, u32[]{:S(2)}) async-start(f32[8,32,512]{2,1,0:T(8,128)} %broadcast_in_dim.72), calls=%async_computation.2 | async-start | bytes 1048576 | tf_op jit(solution)/shard_map/all_to_all | solution.py:141
  123.7 35.5 %all-to-all-start.3 = ((f32[8,128,512]{2,1,0:T(8,128)}), f32[8,128,512]{2,1,0:T(8,128)}, u32[]{:S(2)}, u32[]{:S(2)}) async-start(f32[8,128,512]{2,1,0:T(8,128)} %bitcast.30), calls=%async_computation.3 | async-start | bytes 4194304 | tf_op jit(solution)/shard_map/all_to_all | solution.py:331
  129.1 2.1 collective-permute-start.3
  129.1 30.1 %collective-permute-start.2 = (f32[128,512]{1,0:T(8,128)}, f32[128,512]{1,0:T(8,128)S(1)}, u32[]{:S(2)}, u32[]{:S(2)}) collective-permute-start(f32[128,512]{1,0:T(8,128)} %copy-done.7), channel_id=1, source_target_pairs={{0,0},{1,1},{2,16},{3,17},{4,32},{5,33},{6,48},{7,49},{8,64},{9,65... | collective-permute-start | bytes 786440 | tf_op jit(solution)/shard_map/ppermute | solution.py:159
  131.3 1.0 copy-start.5
  155.3 1.0 copy-start.1
  159.2 1.2 copy-start.2
  164.5 1.4 copy-start.4
  165.9 37.9 %all-to-all-start.5 = ((bf16[8,272,512]{2,1,0:T(8,128)(2,1)}), bf16[8,272,512]{2,1,0:T(8,128)(2,1)}, u32[]{:S(2)}, u32[]{:S(2)}) async-start(bf16[8,272,512]{2,1,0:T(8,128)(2,1)} %copy-done.4), calls=%async_computation.5 | async-start | bytes 4456448 | tf_op jit(solution)/shard_map/all_to_all | solution.py:333
  175.3 7.6 %copy-start.3 = (f32[512,512]{1,0:T(8,128)S(1)}, f32[512,512]{1,0:T(8,128)}, u32[]{:S(2)}) copy-start(f32[512,512]{1,0:T(8,128)} %copy-done.1) | copy-start | bytes 3145732
  180.0 23.7 %collective-permute-start.4 = (bf16[128,512]{1,0:T(8,128)(2,1)S(1)}, bf16[128,512]{1,0:T(8,128)(2,1)S(1)}, u32[]{:S(2)}, u32[]{:S(2)}) collective-permute-start(bf16[128,512]{1,0:T(8,128)(2,1)S(1)} %get-tuple-element.21), channel_id=1, source_target_pairs={{0,0},{1,1},{2,16},{3,17},{4,32},{5,33},{6,48},{7,49},{8,64},{9,65... | collective-permute-start | bytes 393224 | tf_op jit(solution)/shard_map/ppermute | solution.py:159
  205.9 25.1 %all-to-all-start.6 = ((bf16[8,144,512]{2,1,0:T(8,128)(2,1)}), bf16[8,144,512]{2,1,0:T(8,128)(2,1)S(1)}, u32[]{:S(2)}, u32[]{:S(2)}) async-start(bf16[8,144,512]{2,1,0:T(8,128)(2,1)} %broadcast_in_dim.77), calls=%async_computation.6 | async-start | bytes 2359296 | tf_op jit(solution)/shard_map/all_to_all | solution.py:141
  214.8 2.9 %copy-start.6 = (bf16[2048,1024]{1,0:T(8,128)(2,1)S(1)}, bf16[2048,1024]{1,0:T(8,128)(2,1)}, u32[]{:S(2)}) copy-start(bf16[2048,1024]{1,0:T(8,128)(2,1)} %gradient_ref.5) | copy-start | bytes 12582916
  231.0 3.1 %copy-start.9 = (bf16[1024,2048]{1,0:T(8,128)(2,1)S(1)}, bf16[1024,2048]{1,0:T(8,128)(2,1)}, u32[]{:S(2)}) copy-start(bf16[1024,2048]{1,0:T(8,128)(2,1)} %param.8) | copy-start | bytes 12582916
  231.2 3.0 %copy-start.8 = (bf16[8,128,512]{2,1,0:T(8,128)(2,1)S(1)}, bf16[8,128,512]{2,1,0:T(8,128)(2,1)}, u32[]{:S(2)}) copy-start(bf16[8,128,512]{2,1,0:T(8,128)(2,1)} %get-tuple-element.30) | copy-start | bytes 3145732
  231.3 2.8 %collective-permute-start.5 = (bf16[1040,512]{1,0:T(8,128)(2,1)S(1)}, bf16[1040,512]{1,0:T(8,128)(2,1)S(1)}, u32[]{:S(2)}, u32[]{:S(2)}) collective-permute-start(bf16[1040,512]{1,0:T(8,128)(2,1)S(1)} %pad_maximum_fusion), channel_id=1, source_target_pairs={{0,1},{1,0},{2,3},{3,2},{4,5},{5,4},{6,7},{7,6},{8,9},{9,8},{10,11... | collective-permute-start | bytes 3194888 | tf_op jit(solution)/shard_map/ppermute | solution.py:148
  238.5 2.2 copy-start.10
  240.7 16.1 %all-to-all-start.7 = ((bf16[8,32,1024]{2,1,0:T(8,128)(2,1)}), bf16[8,32,1024]{2,1,0:T(8,128)(2,1)S(1)}, u32[]{:S(2)}, u32[]{:S(2)}) async-start(bf16[8,32,1024]{2,1,0:T(8,128)(2,1)} %bitcast.10), calls=%async_computation.7 | async-start | bytes 1048576 | tf_op jit(solution)/shard_map/all_to_all | solution.py:137
